TPU v7x, 128 devices: a whole 4x4x4 slice. The times are simulated.
128 devices in a mesh: tm: 32 (over y, x, core), head: 4 (over z).
Axes of the slice: x: 4, y: 4, z: 4, core: 2. Of those that a mesh axis runs over, the one named last changes fastest.
Arguments:
- queries: bfloat16 [16384, 1024], P('tm', 'head'), may hold values from -5.5 to 5.5
- key_states: bfloat16 [16384, 1024], P('tm', 'head'), may hold values from -5.5 to 5.5
- value_states: bfloat16 [16384, 1024], P('tm', 'head'), may hold values from -6 to 6
- out_weight: bfloat16 [1024, 1024], P('head'), may hold values from -6 to 6
- upstream: bfloat16 [16384, 1024], P('tm'), may hold values from -6 to 6
- windows: int32 [16], P('head'), may hold values from 64 to 256, as said below
- offsets: int32 [16], P('head'), may hold values from 0 to 31
Outputs:
- mixed: bfloat16 [16384, 1024], P('tm')
- grad_queries: bfloat16 [16384, 1024], P('tm', 'head')
- grad_keys: bfloat16 [16384, 1024], P('tm', 'head')
- grad_values: bfloat16 [16384, 1024], P('tm', 'head')
Inputs may be any that keep to these rules, and one draw needn't show every extreme that they name: `windows`: each head's window reaches at most 256 positions to each side, and some head's window is exactly 256.
All inputs are finite; a program needn't handle non-finite values.
Results may differ from a plain program's by a relative error of at most 0.017.
Values may be sent and summed in bfloat16 or wider, within the bound.
No kernel may reach another device: no remote copies, remote signals or barrier semaphores. Data moves between devices by JAX's collectives and lax.ppermute only.
A program may use at most 128 MiB of HBM per device.

v0:
```python
import jax
import jax.numpy as jnp
from jax import lax
from jax.experimental import pallas as pl
from jax.experimental.pallas import tpu as pltpu
from jax.sharding import PartitionSpec as P


F32 = jnp.float32
BF16 = jnp.bfloat16
NEG = -1e30
NT = (((1,), (1,)), ((), ()))
SMEM = pl.BlockSpec(memory_space=pltpu.SMEM)


def sds(shape, dtype):
    return jax.ShapeDtypeStruct(shape, dtype)


def dot(a, b):
    return jnp.dot(a, b, preferred_element_type=F32)


def dot_nt(a, b):
    return lax.dot_general(a, b, NT, preferred_element_type=F32)


def call(body, ins, outs, scratch=(), flops=0, nbytes=0, specs=None, out_specs=None, vmem=24):
    full = lambda x: pl.BlockSpec(x.shape, (lambda *_: (0,) * len(x.shape)))
    specs = specs or [None] * len(ins)
    in_specs = [full(x) if s is None else s for x, s in zip(ins, specs)]
    out_specs = out_specs or [full(o) for o in outs]
    return pl.pallas_call(
        body,
        out_shape=outs,
        grid=(1,),
        in_specs=in_specs,
        out_specs=out_specs,
        scratch_shapes=list(scratch),
        cost_estimate=pl.CostEstimate(flops=int(flops), bytes_accessed=int(nbytes), transcendentals=0),
        compiler_params=pltpu.CompilerParams(vmem_limit_bytes=vmem << 20),
    )(*ins)


def iota(shape, axis):
    return lax.broadcasted_iota(jnp.int32, shape, axis)


def place_row(offset):
    n = iota((1, 256), 1)
    u = jnp.where(n >= 128, 2 * (n - 128) + 1, 4 * (n - 64) + 2)
    u = jnp.where(n >= 64, u, 8 * (n - 32) + 4)
    u = jnp.where(n >= 32, u, 16 * (n - 16) + 8)
    u = jnp.where(n >= 16, u, 32 * (n - 8) + 16)
    u = jnp.where(n >= 8, u, 32 * n)
    return (u + offset) & 255


def rank_row(offset):
    u = (iota((1, 256), 1) - offset) & 255
    n = jnp.where((u & 16) != 0, 8 + (u >> 5), u >> 5)
    n = jnp.where((u & 8) != 0, 16 + (u >> 4), n)
    n = jnp.where((u & 4) != 0, 32 + (u >> 3), n)
    n = jnp.where((u & 2) != 0, 64 + (u >> 2), n)
    return jnp.where((u & 1) != 0, 128 + (u >> 1), n)


def depth(n):
    d = jnp.where(n < 64, 2, 1)
    d = jnp.where(n < 32, 3, d)
    d = jnp.where(n < 16, 4, d)
    return jnp.where(n < 8, 5, d)


def to_depth(offset):
    return (iota((256, 256), 0) == rank_row(offset)).astype(F32).astype(BF16)


def from_depth(offset):
    return (iota((256, 256), 0) == place_row(offset)).astype(F32).astype(BF16)


def lane_first(rows, width=128):
    return (iota((rows, width), 1) % 128) < 64


def zero_pad(x, which):
    z = jnp.zeros_like(x)
    return jnp.concatenate([x, z] if which == 0 else [z, x], axis=0)


def transposed(x):
    return x.T


def parity(tm):
    return tm[0] & 1


def block_rows(tm, which):
    block = (1 - parity(tm)) if which == 0 else parity(tm)
    return pl.ds(pl.multiple_of(256 * block, 256), 256)


def prep_kv(tm, off_hbm, k, v, q, up, w, kvp, c1, n1, x1, x2, qv, upv, wv, kb, vb, off, sem):
    copies = []
    for src, dst in ((k, kb), (v, vb), (q, qv), (up, upv)):
        for which in range(2):
            copies.append(
                pltpu.make_async_copy(
                    src.at[block_rows(tm, which)], dst.at[pl.ds(256 * which, 256)], sem.at[len(copies)]
                )
            )
    copies.append(pltpu.make_async_copy(w, wv, sem.at[8]))
    table = pltpu.make_async_copy(off_hbm, off, sem.at[9])
    table.start()
    for c in copies:
        c.start()
    table.wait()
    perms = [to_depth(off[h]) for h in range(4)]
    for c in copies[:4]:
        c.wait()
    keep = lane_first(256, 256)
    for pair in range(2):
        lanes = slice(pair * 128, pair * 128 + 128)
        for b in range(2):
            rows = slice(b * 256, b * 256 + 256)
            kv = jnp.concatenate([kb[rows, lanes], vb[rows, lanes]], axis=1)
            kvp[rows, pair * 256 : pair * 256 + 256] = jnp.where(
                keep, dot(perms[2 * pair], kv), dot(perms[2 * pair + 1], kv)
            ).astype(BF16)
    x1[0:64] = kvp[0:64]
    x1[64:128] = kvp[256:320]
    x2[0:32] = kvp[0:32]
    x2[32:64] = kvp[256:288]
    c1[...] = kvp[0:384]
    n1[...] = kvp[256:512]
    for c in copies[4:]:
        c.wait()


def prep_qg(off, q, up, w, qt, gt):
    g = dot_nt(w[...], up[...]).astype(BF16)
    qs = (q[...].astype(F32) * 0.125).T.astype(BF16)
    for h in range(4):
        perm = from_depth(off[h])
        hs = slice(64 * h, 64 * h + 64)
        for b in range(2):
            bs = slice(256 * b, 256 * b + 256)
            x = jnp.concatenate([qs[hs, bs], g[hs, bs]], axis=0)
            r = dot(x, perm).astype(BF16)
            qt[b, hs] = r[0:64]
            gt[b, hs] = r[64:128]


def asm_y(kvp, x1, x2a, x2b, y1, y2, both):
    heads = [kvp[0:16], kvp[256:272], x1[0:16], x1[64:80], x2a[0:16], x2a[32:48], x2b[0:16], x2b[32:48]]
    heads = [h.astype(F32) for h in heads]
    y1[...] = jnp.concatenate(heads, axis=0).astype(BF16)
    y2[...] = jnp.concatenate([h[0:8] for h in heads], axis=0).astype(BF16)
    stack(x1, x2a, x2b, both)


def stack(*refs):
    out, at = refs[-1], 0
    for ref in refs[:-1]:
        out[at : at + ref.shape[0]] = ref[...]
        at += ref.shape[0]


def beside(left, right, out):
    out[:, 0 : left.shape[1]] = left[...]
    out[:, left.shape[1] :] = right[...]


def far_rows(bufs, lanes):
    mine_x, other_x, mine_y, other_y = bufs
    out = []
    for mine, other in ((mine_x, other_x), (mine_y, other_y)):
        for half in (slice(0, 128), slice(128, 256)):
            out += [mine[half, lanes], other[half, lanes]]
    return jnp.concatenate(out, axis=0)


def near_count():
    s = (128, 128)
    return jnp.minimum(depth(iota(s, 0)), depth(iota(s, 1))).astype(F32)


def near_keys(kv, c1, lanes):
    return jnp.concatenate([kv[0:128, lanes], kv[256:384, lanes], c1[0:128, lanes], c1[256:384, lanes]], axis=0)


def pair_slices(pair):
    return slice(256 * pair, 256 * pair + 128), slice(256 * pair + 128, 256 * pair + 256)


def side_chunks(which, kv, halo, lanes):
    own, other = slice(256 * which, 256 * which + 256), slice(256 - 256 * which, 512 - 256 * which)
    return [halo[0:256, lanes], kv[own, lanes], kv[other, lanes]]


def both_heads(x, y):
    return jnp.concatenate([zero_pad(x, 0), zero_pad(y, 1)], axis=1)


def fwd_near(which, off, win, tm, qt, kv, c1, *rest):
    if which == 0:
        halo = c1
        pw, p1, acc_out, stat, vt, v1t, dist, sw, s1 = rest
    else:
        halo, pw, p1, acc_out, stat, vt, v1t, dist, sw, s1 = rest
    count = near_count()
    count = jnp.concatenate([count, count], axis=1)
    sign = ((1 - 2 * parity(tm)) * (1 if which == 0 else -1)).astype(F32)
    tops, near_tops = [], []
    for pair in range(2):
        lo, hi = pair_slices(pair)
        heads = [2 * pair, 2 * pair + 1]
        vt[pair] = transposed(jnp.concatenate(side_chunks(which, kv, halo, hi), axis=0))
        v1t[pair] = transposed(near_keys(kv, c1, hi))
        for a, h in enumerate(heads):
            row = place_row(off[h]).astype(F32) * sign
            col = jnp.broadcast_to(row, (128, 256)).T
            dist[pair, :, 256 * a : 256 * a + 256] = jnp.concatenate([col, col], axis=1) - row
        reach = jnp.where(iota((1, 512), 1) < 256, win[heads[0]], win[heads[1]]).astype(F32)
        outer = reach - 256.0
        if which == 1:
            outer = jnp.where((tm[0] == 0) | (tm[0] == 31), -1000.0, outer)
        q0, q1 = [qt[which, 64 * h : 64 * h + 64, :] for h in heads]
        q = both_heads(q0, q1)
        top = None
        for c, keys in enumerate(side_chunks(which, kv, halo, lo)):
            sc = dot(keys, q)
            d = dist[pair]
            ok = (d <= outer, jnp.abs(d) <= reach, d >= 256.0 - reach)[c]
            sc = jnp.where(ok, sc, NEG)
            sw[pair, 256 * c : 256 * c + 256] = sc
            part = jnp.max(sc, axis=0, keepdims=True)
            top = part if top is None else jnp.maximum(top, part)
        sc = dot(near_keys(kv, c1, lo), both_heads(q0[:, 0:128], q1[:, 0:128]))
        s1[pair] = sc
        most = jnp.max(sc, axis=0, keepdims=True)
        first = jnp.maximum(top[:, 0:128], most[:, 0:128])
        second = jnp.maximum(top[:, 256:384], most[:, 128:256])
        near_tops.append(jnp.concatenate([first, second], axis=1))
        tops.append(jnp.concatenate([first, top[:, 128:256], second, top[:, 384:512]], axis=1))
    for pair in range(2):
        total = jnp.zeros((1, 512), F32)
        for c in range(3):
            e = jnp.exp(sw[pair, 256 * c : 256 * c + 256] - tops[pair])
            total += jnp.sum(e, axis=0, keepdims=True)
            pw[pair, 256 * c : 256 * c + 256, :] = e.astype(BF16)
        near_sum = jnp.zeros((1, 256), F32)
        for c in range(4):
            e = count * jnp.exp(s1[pair, 128 * c : 128 * c + 128] - near_tops[pair])
            near_sum += jnp.sum(e, axis=0, keepdims=True)
            p1[pair, 128 * c : 128 * c + 128, :] = e.astype(BF16)
        for a in range(2):
            h = 2 * pair + a
            vh, hs = slice(64 * a, 64 * a + 64), slice(64 * h, 64 * h + 64)
            at = 256 * a
            acc = dot(vt[pair, vh, :], pw[pair, :, at : at + 256])
            near_acc = dot(v1t[pair, vh, :], p1[pair, :, 128 * a : 128 * a + 128])
            acc_out[hs, 0:128] = acc[:, 0:128] + near_acc
            acc_out[hs, 128:256] = acc[:, 128:256]
            stat[h : h + 1, :] = tops[pair][:, at : at + 256]
            stat[4 + h : 5 + h, 0:128] = total[:, at : at + 128] + near_sum[:, 128 * a : 128 * a + 128]
            stat[4 + h : 5 + h, 128:256] = total[:, at + 128 : at + 256]


def far_count(level):
    s = (256 >> level, 128)
    both = jnp.minimum(depth(iota(s, 0)), depth(iota(s, 1) & 63))
    return jnp.maximum(both - level + 1, 0).astype(F32)


def far_lanes(x):
    return jnp.concatenate([x[:, 0:64], x[:, 256:320]], axis=1)


def far_cols(x, hs):
    return jnp.concatenate([x[0, hs, 0:64], x[1, hs, 0:64]], axis=1)


def wide(x, b, filler):
    rows = x.shape[0]
    return jnp.concatenate([x[:, 64 * b : 64 * b + 64], jnp.full((rows, 192), filler, F32)], axis=1)


def unperm_pair(off, pair, src):
    first, second = from_depth(off[2 * pair]), from_depth(off[2 * pair + 1])
    return jnp.where(lane_first(256), dot_nt(first, src), dot_nt(second, src)).astype(BF16)


def fwd_far(off, qt, gt, acc0, acc1, st0, st1, *rest):
    bufs, (pf, attn, stat2, vft, mult, at) = rest[:4], rest[4:]
    for level in range(2, 6):
        n = 256 >> level
        piece = far_count(level)
        for j in range(256 // n):
            mult[256 * (level - 2) + n * j : 256 * (level - 2) + n * j + n] = piece
    cnt = jnp.concatenate([mult[...], mult[...]], axis=1)
    scores, tops, sums, accs = [], [], [], []
    for pair in range(2):
        lo, hi = pair_slices(pair)
        vft[pair] = transposed(far_rows(bufs, hi))
        q = both_heads(*[far_cols(qt, slice(64 * h, 64 * h + 64)) for h in (2 * pair, 2 * pair + 1)])
        sc = jnp.where(cnt > 0, dot(far_rows(bufs, lo), q), NEG)
        tops.append(jnp.max(sc, axis=0, keepdims=True))
        scores.append(sc)
    for pair in range(2):
        e = cnt * jnp.exp(scores[pair] - tops[pair])
        sums.append(jnp.sum(e, axis=0, keepdims=True))
        pf[pair] = e.astype(BF16)
        for a in range(2):
            accs.append(dot(vft[pair, 64 * a : 64 * a + 64, :], pf[pair, :, 128 * a : 128 * a + 128]))
    for pair in range(2):
        for a in range(2):
            h = 2 * pair + a
            hs = slice(64 * h, 64 * h + 64)
            ftop, fsum = [x[pair][:, 128 * a : 128 * a + 128] for x in (tops, sums)]
            for b in range(2):
                bs = slice(256 * b, 256 * b + 256)
                acc_in, stat = (acc0, st0) if b == 0 else (acc1, st1)
                ntop, nsum = stat[h : h + 1, :], stat[4 + h : 5 + h, :]
                ftopw = wide(ftop, b, NEG)
                top = jnp.maximum(ntop, ftopw)
                wn, wf = jnp.exp(ntop - top), jnp.exp(ftopw - top)
                norm = nsum * wn + wide(fsum, b, 0.0) * wf
                acc = acc_in[hs, :] * wn + wide(accs[h], b, 0.0) * wf
                o = (acc / norm).astype(BF16)
                at[hs, bs] = o
                stat2[h : h + 1, bs] = wn / norm
                stat2[4 + h : 5 + h, bs] = wf / norm
                stat2[8 + h : 9 + h, bs] = jnp.sum(
                    gt[b, hs].astype(F32) * o.astype(F32), axis=0, keepdims=True
                )
        for b in range(2):
            bs = slice(256 * b, 256 * b + 256)
            attn[bs, 128 * pair : 128 * pair + 128] = unperm_pair(off, pair, at[128 * pair : 128 * pair + 128, bs])


def scaled(x, by):
    return (x.astype(F32) * by).astype(BF16)


def bwd_far(qt, gt, stat2, pf, *rest):
    bufs, (ret, own_far, dq) = rest[:4], rest[4:]
    keys, dps = [], []
    for pair in range(2):
        lo, hi = pair_slices(pair)
        keys.append(transposed(far_rows(bufs, lo)))
        g = both_heads(*[far_cols(gt, slice(64 * h, 64 * h + 64)) for h in (2 * pair, 2 * pair + 1)])
        dps.append(dot(far_rows(bufs, hi), g))
    for pair in range(2):
        lo, hi = pair_slices(pair)
        heads = (2 * pair, 2 * pair + 1)
        cf = [far_lanes(stat2[4 + h : 5 + h, :]) for h in heads]
        delta = jnp.concatenate([far_lanes(stat2[8 + h : 9 + h, :]) for h in heads], axis=1)
        qs = both_heads(*[scaled(far_cols(qt, slice(64 * h, 64 * h + 64)), c) for h, c in zip(heads, cf)])
        gs = both_heads(*[scaled(far_cols(gt, slice(64 * h, 64 * h + 64)), c) for h, c in zip(heads, cf)])
        ds = (pf[pair].astype(F32) * (dps[pair] - delta)).astype(BF16)
        dk, dv = dot_nt(ds, qs), dot_nt(pf[pair], gs)
        for a, h in enumerate(heads):
            dq[64 * h : 64 * h + 64, :] = (
                dot(keys[pair][64 * a : 64 * a + 64, :], ds[:, 128 * a : 128 * a + 128]) * cf[a]
            )
        for j in range(4):
            mine, theirs = slice(256 * j, 256 * j + 128), slice(256 * j + 128, 256 * j + 256)
            rows = slice(128 * j, 128 * j + 128)
            own_far[rows, lo] = dk[mine]
            own_far[rows, hi] = dv[mine]
            ret[rows, lo] = dk[theirs].astype(BF16)
            ret[rows, hi] = dv[theirs].astype(BF16)


def bwd_keys(qt, gt, stat2, kv, c1, p10, p11, ret, own_near, dq):
    def by_head(x, pair):
        return [
            jnp.concatenate([x[b, 64 * h : 64 * h + 64, 0:128] for b in range(2)], axis=1)
            for h in (2 * pair, 2 * pair + 1)
        ]

    def stats(row):
        return jnp.concatenate([stat2[row : row + 1, 0:128], stat2[row : row + 1, 256:384]], axis=1)

    dps = []
    for pair in range(2):
        dps.append(dot(near_keys(kv, c1, pair_slices(pair)[1]), both_heads(*by_head(gt, pair))))
    for pair in range(2):
        lo, hi = pair_slices(pair)
        heads = (2 * pair, 2 * pair + 1)
        k1t = transposed(near_keys(kv, c1, lo))
        cn = [stats(h) for h in heads]
        delta = jnp.concatenate([stats(8 + h) for h in heads], axis=1)
        left, right = p10[pair], p11[pair]
        p = jnp.concatenate([left[:, 0:128], right[:, 0:128], left[:, 128:256], right[:, 128:256]], axis=1)
        ds = (p.astype(F32) * (dps[pair] - delta)).astype(BF16)
        qs = both_heads(*[scaled(x, c) for x, c in zip(by_head(qt, pair), cn)])
        gs = both_heads(*[scaled(x, c) for x, c in zip(by_head(gt, pair), cn)])
        dk, dv = dot_nt(ds, qs), dot_nt(p, gs)
        for a, h in enumerate(heads):
            dq[64 * h : 64 * h + 64, :] = dot(k1t[64 * a : 64 * a + 64, :], ds[:, 256 * a : 256 * a + 256]) * cn[a]
        own_near[:, lo] = dk[0:256]
        own_near[:, hi] = dv[0:256]
        ret[:, lo] = dk[256:512].astype(BF16)
        ret[:, hi] = dv[256:512].astype(BF16)


def bwd_near(which, off, tm, qt, gt, stat2, kv, halo, pw, dqf, dqn, *rest):
    if which == 1:
        own, halo_out, gq, dqt, dps = rest
    else:
        own_in, own_near, near_s, gq_in, own, halo_out, gq, dqt, dps = rest
        halo_out[256:384] = near_s[128:256]
        gq[block_rows(tm, 1), :] = gq_in[...]
    bs = slice(256 * which, 256 * which + 256)
    ob = slice(256 - 256 * which, 512 - 256 * which)
    for pair in range(2):
        vx = jnp.concatenate(side_chunks(which, kv, halo, pair_slices(pair)[1]), axis=0)
        dps[pair] = dot(vx, both_heads(*[gt[which, 64 * h : 64 * h + 64] for h in (2 * pair, 2 * pair + 1)]))
    for pair in range(2):
        lo, hi = pair_slices(pair)
        heads = (2 * pair, 2 * pair + 1)
        kt = transposed(jnp.concatenate(side_chunks(which, kv, halo, lo), axis=0))
        cn = [stat2[h : h + 1, bs] for h in heads]
        delta = jnp.concatenate([stat2[8 + h : 9 + h, bs] for h in heads], axis=1)
        ds = (pw[pair].astype(F32) * (dps[pair] - delta)).astype(BF16)
        qs = both_heads(*[scaled(qt[which, 64 * h : 64 * h + 64], c) for h, c in zip(heads, cn)])
        gs = both_heads(*[scaled(gt[which, 64 * h : 64 * h + 64], c) for h, c in zip(heads, cn)])
        for a, h in enumerate(heads):
            hs, vh = slice(64 * h, 64 * h + 64), slice(64 * a, 64 * a + 64)
            near = jnp.concatenate(
                [dqn[hs, 128 * which : 128 * which + 128], jnp.zeros((64, 128), F32)], axis=1
            )
            total = dot(kt[vh, :], ds[:, 256 * a : 256 * a + 256]) * cn[a] + near + wide(dqf[hs, :], which, 0.0)
            dqt[pair, vh, :] = (total * 0.125).astype(BF16)
        for lanes, left, right in ((lo, ds, qs), (hi, pw[pair], gs)):
            d = dot_nt(left, right)
            if which == 1:
                halo_out[:, lanes] = d[0:256].astype(BF16)
                own[bs, lanes] = d[256:512]
                own[ob, lanes] = d[512:768]
            else:
                halo_out[0:128, lanes] = (d[0:128] + near_s[0:128, lanes].astype(F32)).astype(BF16)
                halo_out[128:256, lanes] = d[128:256].astype(BF16)
                own[bs, lanes] = d[256:512] + own_in[bs, lanes]
                own[ob, lanes] = d[512:768] + own_in[ob, lanes]
                own[0:128, lanes] += own_near[0:128, lanes]
                own[256:384, lanes] += own_near[128:256, lanes]
        r = unperm_pair(off, pair, dqt[pair])
        if which == 1:
            gq[:, 128 * pair : 128 * pair + 128] = r
        else:
            gq[block_rows(tm, 0), 128 * pair : 128 * pair + 128] = r


def ret_y(own_far, ret, rest, y1, y2a, y2b):
    total = own_far[...] + ret[...].astype(F32)
    rest[...] = total[0:256]
    y1[...] = total[256:384].astype(BF16)
    y2a[...] = total[384:448].astype(BF16)
    y2b[...] = total[448:512].astype(BF16)


def ret_x(rest, y1, y2a, y2b, x1, x2a, x2b):
    deep = y1[...].astype(F32)
    deeper = y2a[...].astype(F32) + y2b[...].astype(F32)
    total = []
    for j, at in enumerate((0, 64, 128, 160, 192, 224)):
        size = 64 if at < 128 else 32
        top = deep[32 + 16 * j : 48 + 16 * j]
        head = rest[at : at + 16] + top
        total += [head[0:8] + deeper[16 + 8 * j : 24 + 8 * j], head[8:16], rest[at + 16 : at + size]]
    x1[...] = jnp.concatenate(total[0:6], axis=0).astype(BF16)
    x2a[...] = jnp.concatenate(total[6:12], axis=0).astype(BF16)
    x2b[...] = jnp.concatenate(total[12:18], axis=0).astype(BF16)


def gather_own(own, hc, hn, y1, y2a, y2b, acc):
    acc[...] = own[...]
    acc[0:384] += hc[...].astype(F32)
    acc[256:512] += hn[...].astype(F32)
    for b in range(2):
        at = 256 * b
        acc[at : at + 16] += y1[16 * b : 16 * b + 16].astype(F32)
        acc[at : at + 8] += (y2a[0:16].astype(F32) + y2b[0:16].astype(F32))[8 * b : 8 * b + 8]


def finish(off, tm, acc, x1, x2a, x2b, gk, gv):
    keep = lane_first(256, 256)
    for pair in range(2):
        first, second = from_depth(off[2 * pair]), from_depth(off[2 * pair + 1])
        lanes = slice(128 * pair, 128 * pair + 128)
        cols = slice(256 * pair, 256 * pair + 256)
        for b in range(2):
            at = 256 * b
            head = acc[at : at + 64, cols] + x1[64 * b : 64 * b + 64, cols].astype(F32)
            deep = x2a[32 * b : 32 * b + 32, cols].astype(F32) + x2b[32 * b : 32 * b + 32, cols].astype(F32)
            x = jnp.concatenate([head[0:32] + deep, head[32:64], acc[at + 64 : at + 256, cols]], axis=0).astype(BF16)
            r = jnp.where(keep, dot(first, x), dot(second, x)).astype(BF16)
            gk[block_rows(tm, b), lanes] = r[:, 0:128]
            gv[block_rows(tm, b), lanes] = r[:, 128:256]


def half_rows(tm, w, out):
    out[...] = w[pl.ds(pl.multiple_of(128 * parity(tm), 128), 128), :]


def asm_w(tm, own, first, other, mine, theirs, out):
    out[0:256] = own[...]
    out[256:512] = first[...]
    out[512:768] = other[...]
    p = parity(tm)
    out[pl.ds(pl.multiple_of(768 + 128 * p, 128), 128), :] = mine[...]
    out[pl.ds(pl.multiple_of(896 - 128 * p, 128), 128), :] = theirs[...]


def project(tm, a01, a23, w, out):
    r = dot(jnp.concatenate([a01[...], a23[...]], axis=1), w[...]).astype(BF16)
    out[block_rows(tm, 0), :] = r[0:256]
    out[block_rows(tm, 1), :] = r[256:512]


def swap(x, axis, mask):
    return lax.ppermute(x, axis, [(i, i ^ mask) for i in range(lax.axis_size(axis))])


def cross(x, masks):
    heads = lax.axis_size("head")
    pairs = []
    for i in range(lax.axis_size("tm")):
        pairs += [(i * heads + z, i * heads + (z ^ masks[i % 2])) for z in range(heads)]
    return lax.ppermute(x, ("tm", "head"), pairs)


def side(x):
    pairs = [(i, i + 1 if i % 2 else i - 1) for i in range(1, lax.axis_size("tm") - 1)]
    return lax.ppermute(x, "tm", pairs)


def bind(f, *args):
    def body(*refs):
        f(*args, *refs)

    return body


def layer(q, k, v, w, up, win, off):
    tm = lax.axis_index("tm").astype(jnp.int32).reshape(1)
    VM = pltpu.VMEM
    hbm = pl.BlockSpec(memory_space=pltpu.HBM)
    rows = lambda n: sds((n, 512), BF16)
    kvp, c1s, n1s, x1s, x2s, qv, upv, wv = call(
        prep_kv, (tm,) + tuple(pltpu.with_memory_space_constraint(x, pltpu.HBM) for x in (off, k, v, q, up, w)),
        [rows(512), rows(384), rows(256), rows(128), rows(64),
         sds((512, 256), BF16), sds((512, 1024), BF16), sds((256, 1024), BF16)],
        specs=[SMEM] + [hbm] * 6,
        scratch=[VM((512, 256), BF16), VM((512, 256), BF16), pltpu.SMEM((4,), jnp.int32), pltpu.SemaphoreType.DMA((10,))],
        flops=3e8, nbytes=3e6,
    )
    x1, x2a, x2b = swap(x1s, "tm", 2), swap(x2s, "tm", 4), swap(x2s, "tm", 6)
    c1 = swap(c1s, "tm", 1)
    n1 = side(n1s)
    w1 = cross(wv, (1, 3))
    (w1h,) = call(half_rows, (tm, w1), [sds((128, 1024), BF16)], specs=[SMEM, None])
    w2 = cross(w1h, (3, 1))
    (w_all,) = call(
        asm_w, (tm, wv, w1, swap(w1, "tm", 1), w2, swap(w2, "tm", 1)),
        [sds((1024, 1024), BF16)], specs=[SMEM] + [None] * 5, nbytes=4e6,
    )
    qt, gt = call(
        prep_qg, (off, qv, upv, wv), [sds((2, 256, 256), BF16), sds((2, 256, 256), BF16)],
        specs=[SMEM] + [None] * 3, flops=6e8, nbytes=3e6,
    )
    near = []
    for which in range(2):
        near.append(
            call(
                bind(fwd_near, which), (off, win, tm, qt, kvp, c1) + ((n1,) if which else ()),
                [sds((2, 768, 512), BF16), sds((2, 512, 256), BF16), sds((256, 256), F32), sds((8, 256), F32)],
                specs=[SMEM] * 3 + [None] * (3 + which),
                scratch=[
                    VM((2, 128, 768), BF16), VM((2, 128, 512), BF16),
                    VM((2, 256, 512), F32), VM((2, 768, 512), F32), VM((2, 512, 256), F32),
                ],
                flops=3e9, nbytes=4e6,
            )
        )
    y1s, y2s, mine_x = call(asm_y, (kvp, x1, x2a, x2b), [rows(128), rows(64), rows(256)])
    y1, y2a, y2b = swap(y1s, "tm", 8), swap(y2s, "tm", 16), swap(y2s, "tm", 24)
    (mine_y,) = call(stack, (y1, y2a, y2b), [rows(256)])
    bufs = (mine_x, swap(mine_x, "tm", 1), mine_y, swap(mine_y, "tm", 1))
    pf, attn, stat2 = call(
        fwd_far, (off, qt, gt, near[0][2], near[1][2], near[0][3], near[1][3], *bufs),
        [sds((2, 1024, 256), BF16), sds((512, 256), BF16), sds((16, 512), F32)],
        specs=[SMEM] + [None] * 10,
        scratch=[VM((2, 128, 1024), BF16), VM((1024, 128), F32), VM((256, 512), BF16)],
        flops=3e9, nbytes=4e6,
    )
    a1 = cross(attn, (1, 3))
    (a01,) = call(beside, (attn, a1), [rows(512)])
    a23 = cross(a01, (3, 1))
    (mixed,) = call(
        project, (tm, a01, a23, w_all), [sds((512, 1024), BF16)],
        specs=[SMEM] + [None] * 3, flops=1e9, nbytes=4e6,
    )
    ret_s, own_far, dqf = call(
        bwd_far, (qt, gt, stat2, pf, *bufs),
        [sds((512, 512), BF16), sds((512, 512), F32), sds((256, 128), F32)],
        flops=4e9, nbytes=5e6,
    )
    ret = swap(ret_s, "tm", 1)
    near_s, own_near, dqn = call(
        bwd_keys, (qt, gt, stat2, kvp, c1, near[0][1], near[1][1]),
        [sds((256, 512), BF16), sds((256, 512), F32), sds((256, 256), F32)],
        flops=4e9, nbytes=5e6,
    )

    def back(which, halo, gq_rows, halo_rows, more):
        return call(
            bind(bwd_near, which), (off, tm, qt, gt, stat2, kvp, halo, near[which][0], dqf, dqn, *more),
            [sds((512, 512), F32), rows(halo_rows), sds((gq_rows, 256), BF16)],
            specs=[SMEM] * 2 + [None] * (8 + len(more)),
            scratch=[VM((2, 128, 256), BF16), VM((2, 768, 512), F32)], flops=4e9, nbytes=4e6,
        )

    own1, hn_s, gq1 = back(1, n1, 256, 256, ())
    own, hc_s, gq = back(0, c1, 512, 384, (own1, own_near, near_s, gq1))
    rest, y1s, y2as, y2bs = call(ret_y, (own_far, ret), [sds((256, 512), F32), rows(128), rows(64), rows(64)])
    yr = [swap(x, "tm", m) for x, m in ((y1s, 8), (y2as, 16), (y2bs, 24))]
    x1s, x2as, x2bs = call(ret_x, (rest, *yr), [rows(128), rows(64), rows(64)])
    xr = [swap(x, "tm", m) for x, m in ((x1s, 2), (x2as, 4), (x2bs, 6))]
    hc, hn = swap(hc_s, "tm", 1), side(hn_s)
    (acc,) = call(gather_own, (own, hc, hn, *yr), [sds((512, 512), F32)], nbytes=3e6)
    gk, gv = call(
        finish, (off, tm, acc, *xr), [sds((512, 256), BF16), sds((512, 256), BF16)],
        specs=[SMEM] * 2 + [None] * 4, flops=3e8, nbytes=3e6,
    )
    return mixed, gq, gk, gv


def solution(mesh):
    placed = (P("tm", "head"),) * 3 + (P("head", None), P("tm", None), P("head"), P("head"))
    return jax.shard_map(
        layer,
        mesh=mesh,
        in_specs=placed,
        out_specs=(P("tm", None), P("tm", "head"), P("tm", "head"), P("tm", "head")),
        check_vma=False,
    )
```

profile of v0, /device:TPU:1, one launch (start us, length us, event | category | flops | bytes accessed | tf_op | source)
XLA Modules:
  0.0 79.1 jit_solution(4299660023569945552)
XLA Ops:
  0.6 1.8 %shard_map.102 = (bf16[512,512]{1,0:T(8,128)(2,1)S(1)}, bf16[384,512]{1,0:T(8,128)(2,1)S(1)}, bf16[256,512]{1,0:T(8,128)(2,1)S(1)}, bf16[128,512]{1,0:T(8,128)(2...) custom-call(s32[1]{0:T(128)} %bitcast.tm.refs_2_.refs_1_, ...), custom_call_target="tpu_custom_call" | custom-call | flops 300000000 | bytes 3000000 | tf_op jit(solution)/shard_map/pallas_call | solution.py:33
  2.5 1.5 %collective-permute-start = (bf16[384,512]{1,0:T(8,128)(2,1)S(1)}, bf16[384,512]{1,0:T(8,128)(2,1)S(1)}, u32[]{:S(2)}, u32[]{:S(2)}) collective-permute-start(bf16[384,512]{1,0:T(8,128)(2,1)S(1)} %get-tuple-element.55), channel_id=1, source_target_pairs={{0,4},{4,0},{8,12},{12,8},{16,20},{20,16},{24,28},{28,24},{32,36},... | collective-permute-start | bytes 1179656 | tf_op jit(solution)/shard_map/ppermute | solution.py:527
  3.9 1.3 %collective-permute-start.2 = (bf16[128,512]{1,0:T(8,128)(2,1)S(1)}, bf16[128,512]{1,0:T(8,128)(2,1)S(1)}, u32[]{:S(2)}, u32[]{:S(2)}) collective-permute-start(bf16[128,512]{1,0:T(8,128)(2,1)S(1)} %get-tuple-element.61), channel_id=1, source_target_pairs={{0,8},{4,12},{8,0},{12,4},{16,24},{20,28},{24,16},{28,20},{32,40},... | collective-permute-start | bytes 393224 | tf_op jit(solution)/shard_map/ppermute | solution.py:527
  5.2 2.5 %collective-permute-start.3 = (bf16[64,512]{1,0:T(8,128)(2,1)S(1)}, bf16[64,512]{1,0:T(8,128)(2,1)S(1)}, u32[]{:S(2)}, u32[]{:S(2)}) collective-permute-start(bf16[64,512]{1,0:T(8,128)(2,1)S(1)} %get-tuple-element.62), channel_id=1, source_target_pairs={{0,16},{4,20},{8,24},{12,28},{16,0},{20,4},{24,8},{28,12},{32,48},... | collective-permute-start | bytes 196616 | tf_op jit(solution)/shard_map/ppermute | solution.py:527
  7.7 0.1 collective-permute-start.4
  7.8 4.8 %collective-permute-done.3.x2a = bf16[64,512]{1,0:T(8,128)(2,1)S(1)} collective-permute-done((bf16[64,512]{1,0:T(8,128)(2,1)S(1)}, bf16[64,512]{1,0:T(8,128)(2,1)S(1)}, u32[]{:S(2)}, u32[]{:S(2)}) %collective-permute-start.3) | collective-permute-done | bytes 65568 | tf_op jit(solution)/shard_map/ppermute | solution.py:527
  12.6 1.2 %collective-permute-done.4.x2b = bf16[64,512]{1,0:T(8,128)(2,1)S(1)} collective-permute-done((bf16[64,512]{1,0:T(8,128)(2,1)S(1)}, bf16[64,512]{1,0:T(8,128)(2,1)S(1)}, u32[]{:S(2)}, u32[]{:S(2)}) %collective-permute-start.4) | collective-permute-done | bytes 65568 | tf_op jit(solution)/shard_map/ppermute | solution.py:527
  13.8 0.0 copy-start.1
  13.8 1.4 %collective-permute-start.6 = (bf16[128,512]{1,0:T(8,128)(2,1)S(1)}, bf16[128,512]{1,0:T(8,128)(2,1)S(1)}, u32[]{:S(2)}, u32[]{:S(2)}) collective-permute-start(bf16[128,512]{1,0:T(8,128)(2,1)S(1)} %get-tuple-element.64), channel_id=1, source_target_pairs={{0,32},{4,36},{8,40},{12,44},{16,48},{20,52},{24,56},{28,60},{32,0... | collective-permute-start | bytes 393224 | tf_op jit(solution)/shard_map/ppermute | solution.py:527
  15.2 2.6 %collective-permute-start.7 = (bf16[64,512]{1,0:T(8,128)(2,1)S(1)}, bf16[64,512]{1,0:T(8,128)(2,1)S(1)}, u32[]{:S(2)}, u32[]{:S(2)}) collective-permute-start(bf16[64,512]{1,0:T(8,128)(2,1)S(1)} %get-tuple-element.65), channel_id=1, source_target_pairs={{0,64},{4,68},{8,72},{12,76},{16,80},{20,84},{24,88},{28,92},{32,9... | collective-permute-start | bytes 196616 | tf_op jit(solution)/shard_map/ppermute | solution.py:527
  17.8 0.0 collective-permute-start.8
  17.8 3.8 %collective-permute-start.12 = (bf16[256,1024]{1,0:T(8,128)(2,1)S(1)}, bf16[256,1024]{1,0:T(8,128)(2,1)S(1)}, u32[]{:S(2)}, u32[]{:S(2)}) collective-permute-start(bf16[256,1024]{1,0:T(8,128)(2,1)S(1)} %get-tuple-element.51.w.own), channel_id=1, source_target_pairs={{0,1},{1,0},{2,3},{3,2},{4,7},{5,6},{6,5},{7,4},{8,9},{9,8},{10,11... | collective-permute-start | bytes 1572872 | tf_op jit(solution)/shard_map/ppermute | solution.py:535
  21.6 1.2 %shard_map.103 = (bf16[2,256,256]{2,1,0:T(8,128)(2,1)S(1)}, bf16[2,256,256]{2,1,0:T(8,128)(2,1)S(1)}) custom-call(s32[4]{0:T(128)S(1)} %copy-done, bf16[512,256]{1,0:T(8,128)(2,1)S(1)} %get-tuple-element.49.q, bf16[512,1024]{1,0:T(8,128)(2,1)S(1)} %get-tuple-element.50.up, bf16[256,1024]{1,0:T(8,128)(2,1)S(1)} %get-tuple-element.51.w.own), custom_call_target="tpu_custom_call" | custom-call | flops 600000000 | bytes 3000000 | tf_op jit(solution)/shard_map/pallas_call | solution.py:33
  22.8 1.9 %collective-permute-start.1 = (bf16[256,512]{1,0:T(8,128)(2,1)S(1)}, bf16[256,512]{1,0:T(8,128)(2,1)S(1)}, u32[]{:S(2)}, u32[]{:S(2)}) collective-permute-start(bf16[256,512]{1,0:T(8,128)(2,1)S(1)} %get-tuple-element.57), channel_id=1, source_target_pairs={{4,8},{8,4},{12,16},{16,12},{20,24},{24,20},{28,32},{32,28},{36,40... | collective-permute-start | bytes 786440 | tf_op jit(solution)/shard_map/ppermute | solution.py:540
  24.7 0.0 collective-permute-done.8.refs_2_
  24.7 0.1 collective-permute-start.5
  24.8 0.0 collective-permute-done.6.refs_0_
  24.9 0.6 collective-permute-start.9
  25.4 0.0 collective-permute-done.refs_5_.c1.refs_6_
  25.5 2.6 %shard_map.104 = (bf16[2,768,512]{2,1,0:T(8,128)(2,1)S(1)}, bf16[2,512,256]{2,1,0:T(8,128)(2,1)S(1)}, f32[256,256]{1,0:T(8,128)S(1)}, f32[8,256]{1,0:T(8,128)S(1)}) custom-call(s32[4]{0:T(128)S(1)} %copy-done, s32[4]{0:T(128)S(1)} %copy-done.1, s32[1]{0:T(128)} %bitcast.tm.refs_2_.refs_1_, bf16[2,256,256]{2,1,0:T(8,128)(2,1)S(1)} %get-tuple-element.52.refs_3_.qt.refs_2_, ...), custom_call_target="tpu_custom_call" | custom-call | flops 3000000000 | bytes 4000000 | tf_op jit(solution)/shard_map/pallas_call | solution.py:33
  28.0 2.5 %collective-permute-done.1.refs_6_ = bf16[256,512]{1,0:T(8,128)(2,1)S(1)} collective-permute-done((bf16[256,512]{1,0:T(8,128)(2,1)S(1)}, bf16[256,512]{1,0:T(8,128)(2,1)S(1)}, u32[]{:S(2)}, u32[]{:S(2)}) %collective-permute-start.1) | collective-permute-done | bytes 262176 | tf_op jit(solution)/shard_map/ppermute | solution.py:540
  30.5 2.5 %shard_map.105 = (bf16[2,768,512]{2,1,0:T(8,128)(2,1)S(1)}, bf16[2,512,256]{2,1,0:T(8,128)(2,1)S(1)}, f32[256,256]{1,0:T(8,128)S(1)}, f32[8,256]{1,0:T(8,128)S(1)}) custom-call(s32[4]{0:T(128)S(1)} %copy-done, s32[4]{0:T(128)S(1)} %copy-done.1, s32[1]{0:T(128)} %bitcast.tm.refs_2_.refs_1_, bf16[2,256,256]{2,1,0:T(8,128)(2,1)S(1)} %get-tuple-element.52.refs_3_.qt.refs_2_, ...), custom_call_target="tpu_custom_call" | custom-call | flops 3000000000 | bytes 4000000 | tf_op jit(solution)/shard_map/pallas_call | solution.py:33
  33.1 2.5 %shard_map.108 = (bf16[2,1024,256]{2,1,0:T(8,128)(2,1)S(1)}, bf16[512,256]{1,0:T(8,128)(2,1)S(1)}, f32[16,512]{1,0:T(8,128)S(1)}) custom-call(s32[4]{0:T(128)S(1)} %copy-done, bf16[2,256,256]{2,1,0:T(8,128)(2,1)S(1)} %get-tuple-element.52.refs_3_.qt.refs_2_, bf16[2,256,256]{2,1,0:T(8,128)(2,1)S(1)} %get-tuple-element.53.gt.refs_3_, ...), custom_call_target="tpu_custom_call" | custom-call | flops 3000000000 | bytes 4000000 | tf_op jit(solution)/shard_map/pallas_call | solution.py:33
  35.5 1.2 %shard_map.113 = (bf16[512,512]{1,0:T(8,128)(2,1)S(1)}, f32[512,512]{1,0:T(8,128)S(1)}, f32[256,128]{1,0:T(8,128)S(1)}) custom-call(bf16[2,256,256]{2,1,0:T(8,128)(2,1)S(1)} %get-tuple-element.52.refs_3_.qt.refs_2_, bf16[2,256,256]{2,1,0:T(8,128)(2,1)S(1)} %get-tuple-element.53.gt.refs_3_, f32[16,512]{1,0:T(8,128)S(1)} %get-tuple-element.67.stat2.refs_4_, ...), custom_call_target="tpu_custom_call" | custom-call | flops 4000000000 | bytes 5000000 | tf_op jit(solution)/shard_map/pallas_call | solution.py:33
  36.8 0.1 collective-permute-start.18
  36.9 2.7 %collective-permute-start.10 = (bf16[512,256]{1,0:T(8,128)(2,1)S(1)}, bf16[512,256]{1,0:T(8,128)(2,1)S(1)}, u32[]{:S(2)}, u32[]{:S(2)}) collective-permute-start(bf16[512,256]{1,0:T(8,128)(2,1)S(1)} %get-tuple-element.66.left), channel_id=1, source_target_pairs={{0,1},{1,0},{2,3},{3,2},{4,7},{5,6},{6,5},{7,4},{8,9},{9,8},{10,11... | collective-permute-start | bytes 786440 | tf_op jit(solution)/shard_map/ppermute | solution.py:535
  39.6 0.1 collective-permute-start.14
  39.7 1.1 %collective-permute-start.13 = (bf16[256,1024]{1,0:T(8,128)(2,1)S(1)}, bf16[256,1024]{1,0:T(8,128)(2,1)S(1)}, u32[]{:S(2)}, u32[]{:S(2)}) collective-permute-start(bf16[256,1024]{1,0:T(8,128)(2,1)S(1)} %collective-permute-done.12.w.first), channel_id=1, source_target_pairs={{0,4},{4,0},{8,12},{12,8},{16,20},{20,16},{24,28},{28,24},{32,36},... | collective-permute-start | bytes 1572872 | tf_op jit(solution)/shard_map/ppermute | solution.py:527
  40.8 1.1 %shard_map.114 = (bf16[256,512]{1,0:T(8,128)(2,1)S(1)}, f32[256,512]{1,0:T(8,128)S(1)}, f32[256,256]{1,0:T(8,128)S(1)}) custom-call(bf16[2,256,256]{2,1,0:T(8,128)(2,1)S(1)} %get-tuple-element.52.refs_3_.qt.refs_2_, bf16[2,256,256]{2,1,0:T(8,128)(2,1)S(1)} %get-tuple-element.53.gt.refs_3_, f32[16,512]{1,0:T(8,128)S(1)} %get-tuple-element.67.stat2.refs_4_, ...), custom_call_target="tpu_custom_call" | custom-call | flops 4000000000 | bytes 5000000 | tf_op jit(solution)/shard_map/pallas_call | solution.py:33
  41.9 2.3 %shard_map.115 = (f32[512,512]{1,0:T(8,128)S(1)}, bf16[256,512]{1,0:T(8,128)(2,1)S(1)}, bf16[256,256]{1,0:T(8,128)(2,1)S(1)}) custom-call(s32[4]{0:T(128)S(1)} %copy-done, s32[1]{0:T(128)} %bitcast.tm.refs_2_.refs_1_, bf16[2,256,256]{2,1,0:T(8,128)(2,1)S(1)} %get-tuple-element.52.refs_3_.qt.refs_2_, bf16[2,256,256]{2,1,0:T(8,128)(2,1)S(1)} %get-tuple-element.53.gt.refs_3_, ...), custom_call_target="tpu_custom_call" | custom-call | flops 4000000000 | bytes 4000000 | tf_op jit(solution)/shard_map/pallas_call | solution.py:33
  44.2 0.5 collective-permute-done.10.right
  44.8 0.4 collective-permute-start.11
  45.1 0.1 shard_map.117
  45.2 4.0 %collective-permute-start.19 = (bf16[128,512]{1,0:T(8,128)(2,1)S(1)}, bf16[128,512]{1,0:T(8,128)(2,1)S(1)}, u32[]{:S(2)}, u32[]{:S(2)}) collective-permute-start(bf16[128,512]{1,0:T(8,128)(2,1)S(1)} %get-tuple-element.85), channel_id=1, source_target_pairs={{0,32},{4,36},{8,40},{12,44},{16,48},{20,52},{24,56},{28,60},{32,0... | collective-permute-start | bytes 393224 | tf_op jit(solution)/shard_map/ppermute | solution.py:527
  49.2 2.6 %collective-permute-start.20 = (bf16[64,512]{1,0:T(8,128)(2,1)S(1)}, bf16[64,512]{1,0:T(8,128)(2,1)S(1)}, u32[]{:S(2)}, u32[]{:S(2)}) collective-permute-start(bf16[64,512]{1,0:T(8,128)(2,1)S(1)} %get-tuple-element.86), channel_id=1, source_target_pairs={{0,64},{4,68},{8,72},{12,76},{16,80},{20,84},{24,88},{28,92},{32,9... | collective-permute-start | bytes 196616 | tf_op jit(solution)/shard_map/ppermute | solution.py:527
  51.8 3.1 %shard_map.116 = (f32[512,512]{1,0:T(8,128)S(1)}, bf16[384,512]{1,0:T(8,128)(2,1)S(1)}, bf16[512,256]{1,0:T(8,128)(2,1)}) custom-call(s32[4]{0:T(128)S(1)} %copy-done, s32[1]{0:T(128)} %bitcast.tm.refs_2_.refs_1_, bf16[2,256,256]{2,1,0:T(8,128)(2,1)S(1)} %get-tuple-element.52.refs_3_.qt.refs_2_, bf16[2,256,256]{2,1,0:T(8,128)(2,1)S(1)} %get-tuple-element.53.gt.refs_3_, ...), custom_call_target="tpu_custom_call" | custom-call | flops 4000000000 | bytes 4000000 | tf_op jit(solution)/shard_map/pallas_call | solution.py:33
  54.9 4.1 %collective-permute-start.16 = (bf16[384,512]{1,0:T(8,128)(2,1)S(1)}, bf16[384,512]{1,0:T(8,128)(2,1)S(1)}, u32[]{:S(2)}, u32[]{:S(2)}) collective-permute-start(bf16[384,512]{1,0:T(8,128)(2,1)S(1)} %get-tuple-element.81), channel_id=1, source_target_pairs={{0,4},{4,0},{8,12},{12,8},{16,20},{20,16},{24,28},{28,24},{32,36},... | collective-permute-start | bytes 1179656 | tf_op jit(solution)/shard_map/ppermute | solution.py:527
  59.1 1.9 %collective-permute-start.17 = (bf16[256,512]{1,0:T(8,128)(2,1)S(1)}, bf16[256,512]{1,0:T(8,128)(2,1)S(1)}, u32[]{:S(2)}, u32[]{:S(2)}) collective-permute-start(bf16[256,512]{1,0:T(8,128)(2,1)S(1)} %get-tuple-element.82), channel_id=1, source_target_pairs={{4,8},{8,4},{12,16},{16,12},{20,24},{24,20},{28,32},{32,28},{36,40... | collective-permute-start | bytes 786440 | tf_op jit(solution)/shard_map/ppermute | solution.py:540
  61.0 0.5 collective-permute-start.15
  61.6 5.2 %collective-permute-done.17.hn = bf16[256,512]{1,0:T(8,128)(2,1)S(1)} collective-permute-done((bf16[256,512]{1,0:T(8,128)(2,1)S(1)}, bf16[256,512]{1,0:T(8,128)(2,1)S(1)}, u32[]{:S(2)}, u32[]{:S(2)}) %collective-permute-start.17) | collective-permute-done | bytes 262176 | tf_op jit(solution)/shard_map/ppermute | solution.py:540
  66.8 3.5 %collective-permute-start.23 = (bf16[64,512]{1,0:T(8,128)(2,1)S(1)}, bf16[64,512]{1,0:T(8,128)(2,1)S(1)}, u32[]{:S(2)}, u32[]{:S(2)}) collective-permute-start(bf16[64,512]{1,0:T(8,128)(2,1)S(1)} %get-tuple-element.90), channel_id=1, source_target_pairs={{0,16},{4,20},{8,24},{12,28},{16,0},{20,4},{24,8},{28,12},{32,48},... | collective-permute-start | bytes 196616 | tf_op jit(solution)/shard_map/ppermute | solution.py:527
  70.3 0.4 collective-permute-start.24
  70.6 0.1 shard_map.111.w
  70.8 0.2 shard_map.118.acc
  71.0 3.2 %collective-permute-done.23.x2a = bf16[64,512]{1,0:T(8,128)(2,1)S(1)} collective-permute-done((bf16[64,512]{1,0:T(8,128)(2,1)S(1)}, bf16[64,512]{1,0:T(8,128)(2,1)S(1)}, u32[]{:S(2)}, u32[]{:S(2)}) %collective-permute-start.23) | collective-permute-done | bytes 65568 | tf_op jit(solution)/shard_map/ppermute | solution.py:527
  74.1 0.9 %collective-permute-done.24.x2b = bf16[64,512]{1,0:T(8,128)(2,1)S(1)} collective-permute-done((bf16[64,512]{1,0:T(8,128)(2,1)S(1)}, bf16[64,512]{1,0:T(8,128)(2,1)S(1)}, u32[]{:S(2)}, u32[]{:S(2)}) %collective-permute-start.24) | collective-permute-done | bytes 65568 | tf_op jit(solution)/shard_map/ppermute | solution.py:527
  75.0 1.8 %shard_map.120 = (bf16[512,256]{1,0:T(8,128)(2,1)}, bf16[512,256]{1,0:T(8,128)(2,1)}) custom-call(s32[4]{0:T(128)S(1)} %copy-done, s32[1]{0:T(128)} %bitcast.tm.refs_2_.refs_1_, f32[512,512]{1,0:T(8,128)S(1)} %shard_map.118.acc, bf16[128,512]{1,0:T(8,128)(2,1)S(1)} %collective-permute-done.22.x1, bf16[64,512]{1,0:T(8,128)(2,1)S(1)} %collective-permute-done.23.x2a, ...), custom_call_target="tpu_custom_call" | custom-call | flops 300000000 | bytes 3000000 | tf_op jit(solution)/shard_map/pallas_call | solution.py:33
  76.8 2.2 %shard_map.112 = bf16[512,1024]{1,0:T(8,128)(2,1)} custom-call(s32[1]{0:T(128)} %bitcast.tm.refs_2_.refs_1_, bf16[512,512]{1,0:T(8,128)(2,1)S(1)} %shard_map.109.a01, bf16[512,512]{1,0:T(8,128)(2,1)S(1)} %collective-permute-done.11.a23, bf16[1024,1024]{1,0:T(8,128)(2,1)S(1)} %shard_map.111.w), custom_call_target="tpu_custom_call" | custom-call | flops 1000000000 | bytes 4000000 | tf_op jit(solution)/shard_map/pallas_call | solution.py:33
  (25 shorter events, 0.2 us)
Async XLA Ops:
  0.6 20.9 %copy-start = (s32[4]{0:T(128)S(1)}, s32[4]{0:T(128)}, u32[]{:S(2)}) copy-start(s32[4]{0:T(128)} %off.5) | copy-start | bytes 52
  2.5 23.0 %collective-permute-start = (bf16[384,512]{1,0:T(8,128)(2,1)S(1)}, bf16[384,512]{1,0:T(8,128)(2,1)S(1)}, u32[]{:S(2)}, u32[]{:S(2)}) collective-permute-start(bf16[384,512]{1,0:T(8,128)(2,1)S(1)} %get-tuple-element.55), channel_id=1, source_target_pairs={{0,4},{4,0},{8,12},{12,8},{16,20},{20,16},{24,28},{28,24},{32,36},... | collective-permute-start | bytes 1179656 | tf_op jit(solution)/shard_map/ppermute | solution.py:527
  3.9 9.9 %collective-permute-start.2 = (bf16[128,512]{1,0:T(8,128)(2,1)S(1)}, bf16[128,512]{1,0:T(8,128)(2,1)S(1)}, u32[]{:S(2)}, u32[]{:S(2)}) collective-permute-start(bf16[128,512]{1,0:T(8,128)(2,1)S(1)} %get-tuple-element.61), channel_id=1, source_target_pairs={{0,8},{4,12},{8,0},{12,4},{16,24},{20,28},{24,16},{28,20},{32,40},... | collective-permute-start | bytes 393224 | tf_op jit(solution)/shard_map/ppermute | solution.py:527
  5.2 7.4 %collective-permute-start.3 = (bf16[64,512]{1,0:T(8,128)(2,1)S(1)}, bf16[64,512]{1,0:T(8,128)(2,1)S(1)}, u32[]{:S(2)}, u32[]{:S(2)}) collective-permute-start(bf16[64,512]{1,0:T(8,128)(2,1)S(1)} %get-tuple-element.62), channel_id=1, source_target_pairs={{0,16},{4,20},{8,24},{12,28},{16,0},{20,4},{24,8},{28,12},{32,48},... | collective-permute-start | bytes 196616 | tf_op jit(solution)/shard_map/ppermute | solution.py:527
  7.7 6.1 %collective-permute-start.4 = (bf16[64,512]{1,0:T(8,128)(2,1)S(1)}, bf16[64,512]{1,0:T(8,128)(2,1)S(1)}, u32[]{:S(2)}, u32[]{:S(2)}) collective-permute-start(bf16[64,512]{1,0:T(8,128)(2,1)S(1)} %get-tuple-element.62), channel_id=1, source_target_pairs={{0,24},{4,28},{8,16},{12,20},{16,8},{20,12},{24,0},{28,4},{32,56},... | collective-permute-start | bytes 196616 | tf_op jit(solution)/shard_map/ppermute | solution.py:527
  13.8 11.6 %copy-start.1 = (s32[4]{0:T(128)S(1)}, s32[4]{0:T(128)}, u32[]{:S(2)}) copy-start(s32[4]{0:T(128)} %refs_1_.3) | copy-start | bytes 52
  13.8 11.0 %collective-permute-start.6 = (bf16[128,512]{1,0:T(8,128)(2,1)S(1)}, bf16[128,512]{1,0:T(8,128)(2,1)S(1)}, u32[]{:S(2)}, u32[]{:S(2)}) collective-permute-start(bf16[128,512]{1,0:T(8,128)(2,1)S(1)} %get-tuple-element.64), channel_id=1, source_target_pairs={{0,32},{4,36},{8,40},{12,44},{16,48},{20,52},{24,56},{28,60},{32,0... | collective-permute-start | bytes 393224 | tf_op jit(solution)/shard_map/ppermute | solution.py:527
  15.2 7.6 %collective-permute-start.7 = (bf16[64,512]{1,0:T(8,128)(2,1)S(1)}, bf16[64,512]{1,0:T(8,128)(2,1)S(1)}, u32[]{:S(2)}, u32[]{:S(2)}) collective-permute-start(bf16[64,512]{1,0:T(8,128)(2,1)S(1)} %get-tuple-element.65), channel_id=1, source_target_pairs={{0,64},{4,68},{8,72},{12,76},{16,80},{20,84},{24,88},{28,92},{32,9... | collective-permute-start | bytes 196616 | tf_op jit(solution)/shard_map/ppermute | solution.py:527
  17.8 6.9 %collective-permute-start.8 = (bf16[64,512]{1,0:T(8,128)(2,1)S(1)}, bf16[64,512]{1,0:T(8,128)(2,1)S(1)}, u32[]{:S(2)}, u32[]{:S(2)}) collective-permute-start(bf16[64,512]{1,0:T(8,128)(2,1)S(1)} %get-tuple-element.65), channel_id=1, source_target_pairs={{0,96},{4,100},{8,104},{12,108},{16,112},{20,116},{24,120},{28,124... | collective-permute-start | bytes 196616 | tf_op jit(solution)/shard_map/ppermute | solution.py:527
  17.8 21.8 %collective-permute-start.12 = (bf16[256,1024]{1,0:T(8,128)(2,1)S(1)}, bf16[256,1024]{1,0:T(8,128)(2,1)S(1)}, u32[]{:S(2)}, u32[]{:S(2)}) collective-permute-start(bf16[256,1024]{1,0:T(8,128)(2,1)S(1)} %get-tuple-element.51.w.own), channel_id=1, source_target_pairs={{0,1},{1,0},{2,3},{3,2},{4,7},{5,6},{6,5},{7,4},{8,9},{9,8},{10,11... | collective-permute-start | bytes 1572872 | tf_op jit(solution)/shard_map/ppermute | solution.py:535
  22.8 7.7 %collective-permute-start.1 = (bf16[256,512]{1,0:T(8,128)(2,1)S(1)}, bf16[256,512]{1,0:T(8,128)(2,1)S(1)}, u32[]{:S(2)}, u32[]{:S(2)}) collective-permute-start(bf16[256,512]{1,0:T(8,128)(2,1)S(1)} %get-tuple-element.57), channel_id=1, source_target_pairs={{4,8},{8,4},{12,16},{16,12},{20,24},{24,20},{28,32},{32,28},{36,40... | collective-permute-start | bytes 786440 | tf_op jit(solution)/shard_map/ppermute | solution.py:540
  24.7 8.3 %collective-permute-start.5 = (bf16[256,512]{1,0:T(8,128)(2,1)S(1)}, bf16[256,512]{1,0:T(8,128)(2,1)S(1)}, u32[]{:S(2)}, u32[]{:S(2)}) collective-permute-start(bf16[256,512]{1,0:T(8,128)(2,1)S(1)} %get-tuple-element.63.rest_0_), channel_id=1, source_target_pairs={{0,4},{4,0},{8,12},{12,8},{16,20},{20,16},{24,28},{28,24},{32,36},... | collective-permute-start | bytes 786440 | tf_op jit(solution)/shard_map/ppermute | solution.py:527
  24.9 8.2 %collective-permute-start.9 = (bf16[256,512]{1,0:T(8,128)(2,1)S(1)}, bf16[256,512]{1,0:T(8,128)(2,1)S(1)}, u32[]{:S(2)}, u32[]{:S(2)}) collective-permute-start(bf16[256,512]{1,0:T(8,128)(2,1)S(1)} %shard_map.107.rest_2_), channel_id=1, source_target_pairs={{0,4},{4,0},{8,12},{12,8},{16,20},{20,16},{24,28},{28,24},{32,36},... | collective-permute-start | bytes 786440 | tf_op jit(solution)/shard_map/ppermute | solution.py:527
  36.8 8.3 %collective-permute-start.18 = (bf16[512,512]{1,0:T(8,128)(2,1)S(1)}, bf16[512,512]{1,0:T(8,128)(2,1)S(1)}, u32[]{:S(2)}, u32[]{:S(2)}) collective-permute-start(bf16[512,512]{1,0:T(8,128)(2,1)S(1)} %get-tuple-element.84), channel_id=1, source_target_pairs={{0,4},{4,0},{8,12},{12,8},{16,20},{20,16},{24,28},{28,24},{32,36},... | collective-permute-start | bytes 1572872 | tf_op jit(solution)/shard_map/ppermute | solution.py:527
  36.9 7.9 %collective-permute-start.10 = (bf16[512,256]{1,0:T(8,128)(2,1)S(1)}, bf16[512,256]{1,0:T(8,128)(2,1)S(1)}, u32[]{:S(2)}, u32[]{:S(2)}) collective-permute-start(bf16[512,256]{1,0:T(8,128)(2,1)S(1)} %get-tuple-element.66.left), channel_id=1, source_target_pairs={{0,1},{1,0},{2,3},{3,2},{4,7},{5,6},{6,5},{7,4},{8,9},{9,8},{10,11... | collective-permute-start | bytes 786440 | tf_op jit(solution)/shard_map/ppermute | solution.py:535
  39.6 12.2 %collective-permute-start.14 = (bf16[128,1024]{1,0:T(8,128)(2,1)S(1)}, bf16[128,1024]{1,0:T(8,128)(2,1)S(1)}, u32[]{:S(2)}, u32[]{:S(2)}) collective-permute-start(bf16[128,1024]{1,0:T(8,128)(2,1)S(1)} %shard_map.110), channel_id=1, source_target_pairs={{0,3},{1,2},{2,1},{3,0},{4,5},{5,4},{6,7},{7,6},{8,11},{9,10},{10,... | collective-permute-start | bytes 786440 | tf_op jit(solution)/shard_map/ppermute | solution.py:535
  39.7 30.6 %collective-permute-start.13 = (bf16[256,1024]{1,0:T(8,128)(2,1)S(1)}, bf16[256,1024]{1,0:T(8,128)(2,1)S(1)}, u32[]{:S(2)}, u32[]{:S(2)}) collective-permute-start(bf16[256,1024]{1,0:T(8,128)(2,1)S(1)} %collective-permute-done.12.w.first), channel_id=1, source_target_pairs={{0,4},{4,0},{8,12},{12,8},{16,20},{20,16},{24,28},{28,24},{32,36},... | collective-permute-start | bytes 1572872 | tf_op jit(solution)/shard_map/ppermute | solution.py:527
  44.8 32.1 %collective-permute-start.11 = (bf16[512,512]{1,0:T(8,128)(2,1)S(1)}, bf16[512,512]{1,0:T(8,128)(2,1)S(1)}, u32[]{:S(2)}, u32[]{:S(2)}) collective-permute-start(bf16[512,512]{1,0:T(8,128)(2,1)S(1)} %shard_map.109.a01), channel_id=1, source_target_pairs={{0,3},{1,2},{2,1},{3,0},{4,5},{5,4},{6,7},{7,6},{8,11},{9,10},{10,... | collective-permute-start | bytes 1572872 | tf_op jit(solution)/shard_map/ppermute | solution.py:535
  45.2 15.8 %collective-permute-start.19 = (bf16[128,512]{1,0:T(8,128)(2,1)S(1)}, bf16[128,512]{1,0:T(8,128)(2,1)S(1)}, u32[]{:S(2)}, u32[]{:S(2)}) collective-permute-start(bf16[128,512]{1,0:T(8,128)(2,1)S(1)} %get-tuple-element.85), channel_id=1, source_target_pairs={{0,32},{4,36},{8,40},{12,44},{16,48},{20,52},{24,56},{28,60},{32,0... | collective-permute-start | bytes 393224 | tf_op jit(solution)/shard_map/ppermute | solution.py:527
  49.2 5.7 %collective-permute-start.20 = (bf16[64,512]{1,0:T(8,128)(2,1)S(1)}, bf16[64,512]{1,0:T(8,128)(2,1)S(1)}, u32[]{:S(2)}, u32[]{:S(2)}) collective-permute-start(bf16[64,512]{1,0:T(8,128)(2,1)S(1)} %get-tuple-element.86), channel_id=1, source_target_pairs={{0,64},{4,68},{8,72},{12,76},{16,80},{20,84},{24,88},{28,92},{32,9... | collective-permute-start | bytes 196616 | tf_op jit(solution)/shard_map/ppermute | solution.py:527
  51.8 7.2 %collective-permute-start.21 = (bf16[64,512]{1,0:T(8,128)(2,1)S(1)}, bf16[64,512]{1,0:T(8,128)(2,1)S(1)}, u32[]{:S(2)}, u32[]{:S(2)}) collective-permute-start(bf16[64,512]{1,0:T(8,128)(2,1)S(1)} %get-tuple-element.87), channel_id=1, source_target_pairs={{0,96},{4,100},{8,104},{12,108},{16,112},{20,116},{24,120},{28,124... | collective-permute-start | bytes 196616 | tf_op jit(solution)/shard_map/ppermute | solution.py:527
  54.9 15.8 %collective-permute-start.16 = (bf16[384,512]{1,0:T(8,128)(2,1)S(1)}, bf16[384,512]{1,0:T(8,128)(2,1)S(1)}, u32[]{:S(2)}, u32[]{:S(2)}) collective-permute-start(bf16[384,512]{1,0:T(8,128)(2,1)S(1)} %get-tuple-element.81), channel_id=1, source_target_pairs={{0,4},{4,0},{8,12},{12,8},{16,20},{20,16},{24,28},{28,24},{32,36},... | collective-permute-start | bytes 1179656 | tf_op jit(solution)/shard_map/ppermute | solution.py:527
  59.1 7.7 %collective-permute-start.17 = (bf16[256,512]{1,0:T(8,128)(2,1)S(1)}, bf16[256,512]{1,0:T(8,128)(2,1)S(1)}, u32[]{:S(2)}, u32[]{:S(2)}) collective-permute-start(bf16[256,512]{1,0:T(8,128)(2,1)S(1)} %get-tuple-element.82), channel_id=1, source_target_pairs={{4,8},{8,4},{12,16},{16,12},{20,24},{24,20},{28,32},{32,28},{36,40... | collective-permute-start | bytes 786440 | tf_op jit(solution)/shard_map/ppermute | solution.py:540
  61.0 5.8 %collective-permute-start.15 = (bf16[128,1024]{1,0:T(8,128)(2,1)S(1)}, bf16[128,1024]{1,0:T(8,128)(2,1)S(1)}, u32[]{:S(2)}, u32[]{:S(2)}) collective-permute-start(bf16[128,1024]{1,0:T(8,128)(2,1)S(1)} %collective-permute-done.14.mine), channel_id=1, source_target_pairs={{0,4},{4,0},{8,12},{12,8},{16,20},{20,16},{24,28},{28,24},{32,36},... | collective-permute-start | bytes 786440 | tf_op jit(solution)/shard_map/ppermute | solution.py:527
  66.8 8.2 %collective-permute-start.22 = (bf16[128,512]{1,0:T(8,128)(2,1)S(1)}, bf16[128,512]{1,0:T(8,128)(2,1)S(1)}, u32[]{:S(2)}, u32[]{:S(2)}) collective-permute-start(bf16[128,512]{1,0:T(8,128)(2,1)S(1)} %get-tuple-element.89), channel_id=1, source_target_pairs={{0,8},{4,12},{8,0},{12,4},{16,24},{20,28},{24,16},{28,20},{32,40},... | collective-permute-start | bytes 393224 | tf_op jit(solution)/shard_map/ppermute | solution.py:527
  66.8 7.4 %collective-permute-start.23 = (bf16[64,512]{1,0:T(8,128)(2,1)S(1)}, bf16[64,512]{1,0:T(8,128)(2,1)S(1)}, u32[]{:S(2)}, u32[]{:S(2)}) collective-permute-start(bf16[64,512]{1,0:T(8,128)(2,1)S(1)} %get-tuple-element.90), channel_id=1, source_target_pairs={{0,16},{4,20},{8,24},{12,28},{16,0},{20,4},{24,8},{28,12},{32,48},... | collective-permute-start | bytes 196616 | tf_op jit(solution)/shard_map/ppermute | solution.py:527
  70.3 4.7 %collective-permute-start.24 = (bf16[64,512]{1,0:T(8,128)(2,1)S(1)}, bf16[64,512]{1,0:T(8,128)(2,1)S(1)}, u32[]{:S(2)}, u32[]{:S(2)}) collective-permute-start(bf16[64,512]{1,0:T(8,128)(2,1)S(1)} %get-tuple-element.91), channel_id=1, source_target_pairs={{0,24},{4,28},{8,16},{12,20},{16,8},{20,12},{24,0},{28,4},{32,56},... | collective-permute-start | bytes 196616 | tf_op jit(solution)/shard_map/ppermute | solution.py:527
where the time goes:
time: 79.2 us; the launch traced here: 79.1 us
  starting transfers between devices  37 us (47%)
  Pallas kernels  23 us (29%)
  waiting for transfers between devices  18.2 us (23%)
  between operations  0.86 us (1%)
    ppermute x19, starting transfers between devices, swap(): lax.ppermute(x, axis, [(i, i ^ mask) for i in range(lax.axis_size(axis))])  26.3 us
    pallas_call x19, Pallas kernels, call(): pl.pallas_call(body, out_shape=outs, grid=(1,), in_specs=in_specs, out_sp...  23 us
    ppermute x19, waiting for transfers between devices, swap(): lax.ppermute(x, axis, [(i, i ^ mask) for i in range(lax.axis_size(axis))])  10.1 us
    ppermute x2, waiting for transfers between devices, side(): return lax.ppermute(x, 'tm', pairs)  7.62 us
    ppermute x4, starting transfers between devices, cross(): return lax.ppermute(x, ('tm', 'head'), pairs)  6.89 us
    ppermute x2, starting transfers between devices, side(): return lax.ppermute(x, 'tm', pairs)  3.83 us
  transfers between devices with their start and end apart: 25, of which 7 were waited for; matrix products, arithmetic and copies ran while one was open for 0% of the time, Pallas kernels for 24%

commit v1 on v0

--- a/solution.py
+++ b/solution.py
@@ -488,20 +488,27 @@
         acc[at : at + 8] += (y2a[0:16].astype(F32) + y2b[0:16].astype(F32))[8 * b : 8 * b + 8]
 
 
-def finish(off, tm, acc, x1, x2a, x2b, gk, gv):
+def finish(off, tm, acc, x1, x2a, x2b, gk, gv, kb, vb, sem):
     keep = lane_first(256, 256)
-    for pair in range(2):
-        first, second = from_depth(off[2 * pair]), from_depth(off[2 * pair + 1])
-        lanes = slice(128 * pair, 128 * pair + 128)
-        cols = slice(256 * pair, 256 * pair + 256)
-        for b in range(2):
-            at = 256 * b
+    perms = [from_depth(off[h]) for h in range(4)]
+    copies = []
+    for b in range(2):
+        at = 256 * b
+        rows = slice(at, at + 256)
+        for pair in range(2):
+            lanes = slice(128 * pair, 128 * pair + 128)
+            cols = slice(256 * pair, 256 * pair + 256)
             head = acc[at : at + 64, cols] + x1[64 * b : 64 * b + 64, cols].astype(F32)
             deep = x2a[32 * b : 32 * b + 32, cols].astype(F32) + x2b[32 * b : 32 * b + 32, cols].astype(F32)
             x = jnp.concatenate([head[0:32] + deep, head[32:64], acc[at + 64 : at + 256, cols]], axis=0).astype(BF16)
-            r = jnp.where(keep, dot(first, x), dot(second, x)).astype(BF16)
-            gk[block_rows(tm, b), lanes] = r[:, 0:128]
-            gv[block_rows(tm, b), lanes] = r[:, 128:256]
+            r = jnp.where(keep, dot(perms[2 * pair], x), dot(perms[2 * pair + 1], x)).astype(BF16)
+            kb[rows, lanes] = r[:, 0:128]
+            vb[rows, lanes] = r[:, 128:256]
+        for src, dst in ((kb, gk), (vb, gv)):
+            copies.append(pltpu.make_async_copy(src.at[rows], dst.at[block_rows(tm, b)], sem.at[len(copies)]))
+            copies[-1].start()
+    for c in copies:
+        c.wait()
 
 
 def half_rows(tm, w, out):
@@ -517,10 +524,18 @@
     out[pl.ds(pl.multiple_of(896 - 128 * p, 128), 128), :] = theirs[...]
 
 
-def project(tm, a01, a23, w, out):
-    r = dot(jnp.concatenate([a01[...], a23[...]], axis=1), w[...]).astype(BF16)
-    out[block_rows(tm, 0), :] = r[0:256]
-    out[block_rows(tm, 1), :] = r[256:512]
+def project(tm, a01, a23, w, out, buf, sem):
+    a = jnp.concatenate([a01[...], a23[...]], axis=1)
+    copies = []
+    for c in range(4):
+        cols = slice(256 * c, 256 * c + 256)
+        buf[:, cols] = dot(a, w[:, cols]).astype(BF16)
+        for b in range(2):
+            src = buf.at[256 * b : 256 * b + 256, cols]
+            copies.append(pltpu.make_async_copy(src, out.at[block_rows(tm, b), cols], sem.at[len(copies)]))
+            copies[-1].start()
+    for c in copies:
+        c.wait()
 
 
 def swap(x, axis, mask):
@@ -604,7 +619,8 @@
     a23 = cross(a01, (3, 1))
     (mixed,) = call(
         project, (tm, a01, a23, w_all), [sds((512, 1024), BF16)],
-        specs=[SMEM] + [None] * 3, flops=1e9, nbytes=4e6,
+        specs=[SMEM] + [None] * 3, out_specs=[pl.BlockSpec(memory_space=pl.ANY)],
+        scratch=[VM((512, 1024), BF16), pltpu.SemaphoreType.DMA((8,))], flops=1e9, nbytes=4e6,
     )
     ret_s, own_far, dqf = call(
         bwd_far, (qt, gt, stat2, pf, *bufs),
@@ -636,6 +652,8 @@
     (acc,) = call(gather_own, (own, hc, hn, *yr), [sds((512, 512), F32)], nbytes=3e6)
     gk, gv = call(
         finish, (off, tm, acc, *xr), [sds((512, 256), BF16), sds((512, 256), BF16)],
+        out_specs=[pl.BlockSpec(memory_space=pl.ANY)] * 2,
+        scratch=[VM((512, 256), BF16), VM((512, 256), BF16), pltpu.SemaphoreType.DMA((4,))],
         specs=[SMEM] * 2 + [None] * 4, flops=3e8, nbytes=3e6,
     )
     return mixed, gq, gk, gv

time: 79.2 us -> 79.3 us (level)
  no operation moved by 1% of the time
where the time goes in v1:
time: 79.3 us; the launch traced here: 79.1 us
  starting transfers between devices  37 us (47%)
  Pallas kernels  22.9 us (29%)
  waiting for transfers between devices  18.2 us (23%)
  between operations  1.04 us (1%)
    ppermute x19, starting transfers between devices, swap(): lax.ppermute(x, axis, [(i, i ^ mask) for i in range(lax.axis_size(axis))])  26.3 us
    pallas_call x19, Pallas kernels, call(): pl.pallas_call(body, out_shape=outs, grid=(1,), in_specs=in_specs, out_sp...  22.9 us
    ppermute x19, waiting for transfers between devices, swap(): lax.ppermute(x, axis, [(i, i ^ mask) for i in range(lax.axis_size(axis))])  10.1 us
    ppermute x2, waiting for transfers between devices, side(): return lax.ppermute(x, 'tm', pairs)  7.62 us
    ppermute x4, starting transfers between devices, cross(): return lax.ppermute(x, ('tm', 'head'), pairs)  6.89 us
    ppermute x2, starting transfers between devices, side(): return lax.ppermute(x, 'tm', pairs)  3.83 us
  transfers between devices with their start and end apart: 25, of which 7 were waited for; matrix products, arithmetic and copies ran while one was open for 0% of the time, Pallas kernels for 24%

profile of v1, /device:TPU:1, one launch (start us, length us, event | category | flops | bytes accessed | tf_op | source)
XLA Modules:
  0.0 79.1 jit_solution(13458646738153627964)
XLA Ops:
  0.6 1.8 %shard_map.102 = (bf16[512,512]{1,0:T(8,128)(2,1)S(1)}, bf16[384,512]{1,0:T(8,128)(2,1)S(1)}, bf16[256,512]{1,0:T(8,128)(2,1)S(1)}, bf16[128,512]{1,0:T(8,128)(2...) custom-call(s32[1]{0:T(128)} %bitcast.tm.refs_2_.refs_1_, ...), custom_call_target="tpu_custom_call" | custom-call | flops 300000000 | bytes 3000000 | tf_op jit(solution)/shard_map/pallas_call | solution.py:33
  2.5 1.5 %collective-permute-start = (bf16[384,512]{1,0:T(8,128)(2,1)S(1)}, bf16[384,512]{1,0:T(8,128)(2,1)S(1)}, u32[]{:S(2)}, u32[]{:S(2)}) collective-permute-start(bf16[384,512]{1,0:T(8,128)(2,1)S(1)} %get-tuple-element.55), channel_id=1, source_target_pairs={{0,4},{4,0},{8,12},{12,8},{16,20},{20,16},{24,28},{28,24},{32,36},... | collective-permute-start | bytes 1179656 | tf_op jit(solution)/shard_map/ppermute | solution.py:542
  3.9 1.3 %collective-permute-start.2 = (bf16[128,512]{1,0:T(8,128)(2,1)S(1)}, bf16[128,512]{1,0:T(8,128)(2,1)S(1)}, u32[]{:S(2)}, u32[]{:S(2)}) collective-permute-start(bf16[128,512]{1,0:T(8,128)(2,1)S(1)} %get-tuple-element.61), channel_id=1, source_target_pairs={{0,8},{4,12},{8,0},{12,4},{16,24},{20,28},{24,16},{28,20},{32,40},... | collective-permute-start | bytes 393224 | tf_op jit(solution)/shard_map/ppermute | solution.py:542
  5.2 2.5 %collective-permute-start.3 = (bf16[64,512]{1,0:T(8,128)(2,1)S(1)}, bf16[64,512]{1,0:T(8,128)(2,1)S(1)}, u32[]{:S(2)}, u32[]{:S(2)}) collective-permute-start(bf16[64,512]{1,0:T(8,128)(2,1)S(1)} %get-tuple-element.62), channel_id=1, source_target_pairs={{0,16},{4,20},{8,24},{12,28},{16,0},{20,4},{24,8},{28,12},{32,48},... | collective-permute-start | bytes 196616 | tf_op jit(solution)/shard_map/ppermute | solution.py:542
  7.7 0.1 collective-permute-start.4
  7.8 4.8 %collective-permute-done.3.x2a = bf16[64,512]{1,0:T(8,128)(2,1)S(1)} collective-permute-done((bf16[64,512]{1,0:T(8,128)(2,1)S(1)}, bf16[64,512]{1,0:T(8,128)(2,1)S(1)}, u32[]{:S(2)}, u32[]{:S(2)}) %collective-permute-start.3) | collective-permute-done | bytes 65568 | tf_op jit(solution)/shard_map/ppermute | solution.py:542
  12.6 1.2 %collective-permute-done.4.x2b = bf16[64,512]{1,0:T(8,128)(2,1)S(1)} collective-permute-done((bf16[64,512]{1,0:T(8,128)(2,1)S(1)}, bf16[64,512]{1,0:T(8,128)(2,1)S(1)}, u32[]{:S(2)}, u32[]{:S(2)}) %collective-permute-start.4) | collective-permute-done | bytes 65568 | tf_op jit(solution)/shard_map/ppermute | solution.py:542
  13.8 0.0 copy-start.1
  13.8 1.4 %collective-permute-start.6 = (bf16[128,512]{1,0:T(8,128)(2,1)S(1)}, bf16[128,512]{1,0:T(8,128)(2,1)S(1)}, u32[]{:S(2)}, u32[]{:S(2)}) collective-permute-start(bf16[128,512]{1,0:T(8,128)(2,1)S(1)} %get-tuple-element.64), channel_id=1, source_target_pairs={{0,32},{4,36},{8,40},{12,44},{16,48},{20,52},{24,56},{28,60},{32,0... | collective-permute-start | bytes 393224 | tf_op jit(solution)/shard_map/ppermute | solution.py:542
  15.2 2.6 %collective-permute-start.7 = (bf16[64,512]{1,0:T(8,128)(2,1)S(1)}, bf16[64,512]{1,0:T(8,128)(2,1)S(1)}, u32[]{:S(2)}, u32[]{:S(2)}) collective-permute-start(bf16[64,512]{1,0:T(8,128)(2,1)S(1)} %get-tuple-element.65), channel_id=1, source_target_pairs={{0,64},{4,68},{8,72},{12,76},{16,80},{20,84},{24,88},{28,92},{32,9... | collective-permute-start | bytes 196616 | tf_op jit(solution)/shard_map/ppermute | solution.py:542
  17.8 0.0 collective-permute-start.8
  17.8 3.8 %collective-permute-start.12 = (bf16[256,1024]{1,0:T(8,128)(2,1)S(1)}, bf16[256,1024]{1,0:T(8,128)(2,1)S(1)}, u32[]{:S(2)}, u32[]{:S(2)}) collective-permute-start(bf16[256,1024]{1,0:T(8,128)(2,1)S(1)} %get-tuple-element.51.w.own), channel_id=1, source_target_pairs={{0,1},{1,0},{2,3},{3,2},{4,7},{5,6},{6,5},{7,4},{8,9},{9,8},{10,11... | collective-permute-start | bytes 1572872 | tf_op jit(solution)/shard_map/ppermute | solution.py:550
  21.6 1.2 %shard_map.103 = (bf16[2,256,256]{2,1,0:T(8,128)(2,1)S(1)}, bf16[2,256,256]{2,1,0:T(8,128)(2,1)S(1)}) custom-call(s32[4]{0:T(128)S(1)} %copy-done, bf16[512,256]{1,0:T(8,128)(2,1)S(1)} %get-tuple-element.49.q, bf16[512,1024]{1,0:T(8,128)(2,1)S(1)} %get-tuple-element.50.up, bf16[256,1024]{1,0:T(8,128)(2,1)S(1)} %get-tuple-element.51.w.own), custom_call_target="tpu_custom_call" | custom-call | flops 600000000 | bytes 3000000 | tf_op jit(solution)/shard_map/pallas_call | solution.py:33
  22.8 1.9 %collective-permute-start.1 = (bf16[256,512]{1,0:T(8,128)(2,1)S(1)}, bf16[256,512]{1,0:T(8,128)(2,1)S(1)}, u32[]{:S(2)}, u32[]{:S(2)}) collective-permute-start(bf16[256,512]{1,0:T(8,128)(2,1)S(1)} %get-tuple-element.57), channel_id=1, source_target_pairs={{4,8},{8,4},{12,16},{16,12},{20,24},{24,20},{28,32},{32,28},{36,40... | collective-permute-start | bytes 786440 | tf_op jit(solution)/shard_map/ppermute | solution.py:555
  24.7 0.0 collective-permute-done.8.refs_2_
  24.7 0.1 collective-permute-start.5
  24.8 0.0 collective-permute-done.6.refs_0_
  24.9 0.6 collective-permute-start.9
  25.4 0.0 collective-permute-done.refs_5_.c1.refs_6_
  25.5 2.6 %shard_map.104 = (bf16[2,768,512]{2,1,0:T(8,128)(2,1)S(1)}, bf16[2,512,256]{2,1,0:T(8,128)(2,1)S(1)}, f32[256,256]{1,0:T(8,128)S(1)}, f32[8,256]{1,0:T(8,128)S(1)}) custom-call(s32[4]{0:T(128)S(1)} %copy-done, s32[4]{0:T(128)S(1)} %copy-done.1, s32[1]{0:T(128)} %bitcast.tm.refs_2_.refs_1_, bf16[2,256,256]{2,1,0:T(8,128)(2,1)S(1)} %get-tuple-element.52.refs_3_.qt.refs_2_, ...), custom_call_target="tpu_custom_call" | custom-call | flops 3000000000 | bytes 4000000 | tf_op jit(solution)/shard_map/pallas_call | solution.py:33
  28.0 2.5 %collective-permute-done.1.refs_6_ = bf16[256,512]{1,0:T(8,128)(2,1)S(1)} collective-permute-done((bf16[256,512]{1,0:T(8,128)(2,1)S(1)}, bf16[256,512]{1,0:T(8,128)(2,1)S(1)}, u32[]{:S(2)}, u32[]{:S(2)}) %collective-permute-start.1) | collective-permute-done | bytes 262176 | tf_op jit(solution)/shard_map/ppermute | solution.py:555
  30.5 2.5 %shard_map.105 = (bf16[2,768,512]{2,1,0:T(8,128)(2,1)S(1)}, bf16[2,512,256]{2,1,0:T(8,128)(2,1)S(1)}, f32[256,256]{1,0:T(8,128)S(1)}, f32[8,256]{1,0:T(8,128)S(1)}) custom-call(s32[4]{0:T(128)S(1)} %copy-done, s32[4]{0:T(128)S(1)} %copy-done.1, s32[1]{0:T(128)} %bitcast.tm.refs_2_.refs_1_, bf16[2,256,256]{2,1,0:T(8,128)(2,1)S(1)} %get-tuple-element.52.refs_3_.qt.refs_2_, ...), custom_call_target="tpu_custom_call" | custom-call | flops 3000000000 | bytes 4000000 | tf_op jit(solution)/shard_map/pallas_call | solution.py:33
  33.1 2.5 %shard_map.108 = (bf16[2,1024,256]{2,1,0:T(8,128)(2,1)S(1)}, bf16[512,256]{1,0:T(8,128)(2,1)S(1)}, f32[16,512]{1,0:T(8,128)S(1)}) custom-call(s32[4]{0:T(128)S(1)} %copy-done, bf16[2,256,256]{2,1,0:T(8,128)(2,1)S(1)} %get-tuple-element.52.refs_3_.qt.refs_2_, bf16[2,256,256]{2,1,0:T(8,128)(2,1)S(1)} %get-tuple-element.53.gt.refs_3_, ...), custom_call_target="tpu_custom_call" | custom-call | flops 3000000000 | bytes 4000000 | tf_op jit(solution)/shard_map/pallas_call | solution.py:33
  35.5 1.2 %shard_map.113 = (bf16[512,512]{1,0:T(8,128)(2,1)S(1)}, f32[512,512]{1,0:T(8,128)S(1)}, f32[256,128]{1,0:T(8,128)S(1)}) custom-call(bf16[2,256,256]{2,1,0:T(8,128)(2,1)S(1)} %get-tuple-element.52.refs_3_.qt.refs_2_, bf16[2,256,256]{2,1,0:T(8,128)(2,1)S(1)} %get-tuple-element.53.gt.refs_3_, f32[16,512]{1,0:T(8,128)S(1)} %get-tuple-element.67.stat2.refs_4_, ...), custom_call_target="tpu_custom_call" | custom-call | flops 4000000000 | bytes 5000000 | tf_op jit(solution)/shard_map/pallas_call | solution.py:33
  36.8 0.1 collective-permute-start.18
  36.9 2.7 %collective-permute-start.10 = (bf16[512,256]{1,0:T(8,128)(2,1)S(1)}, bf16[512,256]{1,0:T(8,128)(2,1)S(1)}, u32[]{:S(2)}, u32[]{:S(2)}) collective-permute-start(bf16[512,256]{1,0:T(8,128)(2,1)S(1)} %get-tuple-element.66.left), channel_id=1, source_target_pairs={{0,1},{1,0},{2,3},{3,2},{4,7},{5,6},{6,5},{7,4},{8,9},{9,8},{10,11... | collective-permute-start | bytes 786440 | tf_op jit(solution)/shard_map/ppermute | solution.py:550
  39.6 0.1 collective-permute-start.14
  39.7 1.1 %collective-permute-start.13 = (bf16[256,1024]{1,0:T(8,128)(2,1)S(1)}, bf16[256,1024]{1,0:T(8,128)(2,1)S(1)}, u32[]{:S(2)}, u32[]{:S(2)}) collective-permute-start(bf16[256,1024]{1,0:T(8,128)(2,1)S(1)} %collective-permute-done.12.w.first), channel_id=1, source_target_pairs={{0,4},{4,0},{8,12},{12,8},{16,20},{20,16},{24,28},{28,24},{32,36},... | collective-permute-start | bytes 1572872 | tf_op jit(solution)/shard_map/ppermute | solution.py:542
  40.8 1.1 %shard_map.114 = (bf16[256,512]{1,0:T(8,128)(2,1)S(1)}, f32[256,512]{1,0:T(8,128)S(1)}, f32[256,256]{1,0:T(8,128)S(1)}) custom-call(bf16[2,256,256]{2,1,0:T(8,128)(2,1)S(1)} %get-tuple-element.52.refs_3_.qt.refs_2_, bf16[2,256,256]{2,1,0:T(8,128)(2,1)S(1)} %get-tuple-element.53.gt.refs_3_, f32[16,512]{1,0:T(8,128)S(1)} %get-tuple-element.67.stat2.refs_4_, ...), custom_call_target="tpu_custom_call" | custom-call | flops 4000000000 | bytes 5000000 | tf_op jit(solution)/shard_map/pallas_call | solution.py:33
  41.9 2.3 %shard_map.115 = (f32[512,512]{1,0:T(8,128)S(1)}, bf16[256,512]{1,0:T(8,128)(2,1)S(1)}, bf16[256,256]{1,0:T(8,128)(2,1)S(1)}) custom-call(s32[4]{0:T(128)S(1)} %copy-done, s32[1]{0:T(128)} %bitcast.tm.refs_2_.refs_1_, bf16[2,256,256]{2,1,0:T(8,128)(2,1)S(1)} %get-tuple-element.52.refs_3_.qt.refs_2_, bf16[2,256,256]{2,1,0:T(8,128)(2,1)S(1)} %get-tuple-element.53.gt.refs_3_, ...), custom_call_target="tpu_custom_call" | custom-call | flops 4000000000 | bytes 4000000 | tf_op jit(solution)/shard_map/pallas_call | solution.py:33
  44.2 0.5 collective-permute-done.10.right
  44.8 0.4 collective-permute-start.11
  45.1 0.1 shard_map.117
  45.2 4.0 %collective-permute-start.19 = (bf16[128,512]{1,0:T(8,128)(2,1)S(1)}, bf16[128,512]{1,0:T(8,128)(2,1)S(1)}, u32[]{:S(2)}, u32[]{:S(2)}) collective-permute-start(bf16[128,512]{1,0:T(8,128)(2,1)S(1)} %get-tuple-element.85), channel_id=1, source_target_pairs={{0,32},{4,36},{8,40},{12,44},{16,48},{20,52},{24,56},{28,60},{32,0... | collective-permute-start | bytes 393224 | tf_op jit(solution)/shard_map/ppermute | solution.py:542
  49.2 2.6 %collective-permute-start.20 = (bf16[64,512]{1,0:T(8,128)(2,1)S(1)}, bf16[64,512]{1,0:T(8,128)(2,1)S(1)}, u32[]{:S(2)}, u32[]{:S(2)}) collective-permute-start(bf16[64,512]{1,0:T(8,128)(2,1)S(1)} %get-tuple-element.86), channel_id=1, source_target_pairs={{0,64},{4,68},{8,72},{12,76},{16,80},{20,84},{24,88},{28,92},{32,9... | collective-permute-start | bytes 196616 | tf_op jit(solution)/shard_map/ppermute | solution.py:542
  51.8 3.1 %shard_map.116 = (f32[512,512]{1,0:T(8,128)S(1)}, bf16[384,512]{1,0:T(8,128)(2,1)S(1)}, bf16[512,256]{1,0:T(8,128)(2,1)}) custom-call(s32[4]{0:T(128)S(1)} %copy-done, s32[1]{0:T(128)} %bitcast.tm.refs_2_.refs_1_, bf16[2,256,256]{2,1,0:T(8,128)(2,1)S(1)} %get-tuple-element.52.refs_3_.qt.refs_2_, bf16[2,256,256]{2,1,0:T(8,128)(2,1)S(1)} %get-tuple-element.53.gt.refs_3_, ...), custom_call_target="tpu_custom_call" | custom-call | flops 4000000000 | bytes 4000000 | tf_op jit(solution)/shard_map/pallas_call | solution.py:33
  54.9 4.1 %collective-permute-start.16 = (bf16[384,512]{1,0:T(8,128)(2,1)S(1)}, bf16[384,512]{1,0:T(8,128)(2,1)S(1)}, u32[]{:S(2)}, u32[]{:S(2)}) collective-permute-start(bf16[384,512]{1,0:T(8,128)(2,1)S(1)} %get-tuple-element.81), channel_id=1, source_target_pairs={{0,4},{4,0},{8,12},{12,8},{16,20},{20,16},{24,28},{28,24},{32,36},... | collective-permute-start | bytes 1179656 | tf_op jit(solution)/shard_map/ppermute | solution.py:542
  59.1 1.9 %collective-permute-start.17 = (bf16[256,512]{1,0:T(8,128)(2,1)S(1)}, bf16[256,512]{1,0:T(8,128)(2,1)S(1)}, u32[]{:S(2)}, u32[]{:S(2)}) collective-permute-start(bf16[256,512]{1,0:T(8,128)(2,1)S(1)} %get-tuple-element.82), channel_id=1, source_target_pairs={{4,8},{8,4},{12,16},{16,12},{20,24},{24,20},{28,32},{32,28},{36,40... | collective-permute-start | bytes 786440 | tf_op jit(solution)/shard_map/ppermute | solution.py:555
  61.0 0.5 collective-permute-start.15
  61.6 5.2 %collective-permute-done.17.hn = bf16[256,512]{1,0:T(8,128)(2,1)S(1)} collective-permute-done((bf16[256,512]{1,0:T(8,128)(2,1)S(1)}, bf16[256,512]{1,0:T(8,128)(2,1)S(1)}, u32[]{:S(2)}, u32[]{:S(2)}) %collective-permute-start.17) | collective-permute-done | bytes 262176 | tf_op jit(solution)/shard_map/ppermute | solution.py:555
  66.8 3.5 %collective-permute-start.23 = (bf16[64,512]{1,0:T(8,128)(2,1)S(1)}, bf16[64,512]{1,0:T(8,128)(2,1)S(1)}, u32[]{:S(2)}, u32[]{:S(2)}) collective-permute-start(bf16[64,512]{1,0:T(8,128)(2,1)S(1)} %get-tuple-element.90), channel_id=1, source_target_pairs={{0,16},{4,20},{8,24},{12,28},{16,0},{20,4},{24,8},{28,12},{32,48},... | collective-permute-start | bytes 196616 | tf_op jit(solution)/shard_map/ppermute | solution.py:542
  70.3 0.4 collective-permute-start.24
  70.6 0.1 shard_map.111.w
  70.8 0.2 shard_map.118.acc
  71.0 3.2 %collective-permute-done.23.x2a = bf16[64,512]{1,0:T(8,128)(2,1)S(1)} collective-permute-done((bf16[64,512]{1,0:T(8,128)(2,1)S(1)}, bf16[64,512]{1,0:T(8,128)(2,1)S(1)}, u32[]{:S(2)}, u32[]{:S(2)}) %collective-permute-start.23) | collective-permute-done | bytes 65568 | tf_op jit(solution)/shard_map/ppermute | solution.py:542
  74.1 0.9 %collective-permute-done.24.x2b = bf16[64,512]{1,0:T(8,128)(2,1)S(1)} collective-permute-done((bf16[64,512]{1,0:T(8,128)(2,1)S(1)}, bf16[64,512]{1,0:T(8,128)(2,1)S(1)}, u32[]{:S(2)}, u32[]{:S(2)}) %collective-permute-start.24) | collective-permute-done | bytes 65568 | tf_op jit(solution)/shard_map/ppermute | solution.py:542
  75.0 1.7 %shard_map.120 = (bf16[512,256]{1,0:T(8,128)(2,1)}, bf16[512,256]{1,0:T(8,128)(2,1)}) custom-call(s32[4]{0:T(128)S(1)} %copy-done, s32[1]{0:T(128)} %bitcast.tm.refs_2_.refs_1_, f32[512,512]{1,0:T(8,128)S(1)} %shard_map.118.acc, bf16[128,512]{1,0:T(8,128)(2,1)S(1)} %collective-permute-done.22.x1, bf16[64,512]{1,0:T(8,128)(2,1)S(1)} %collective-permute-done.23.x2a, ...), custom_call_target="tpu_custom_call" | custom-call | flops 300000000 | bytes 3000000 | tf_op jit(solution)/shard_map/pallas_call | solution.py:33
  76.8 2.2 %shard_map.112 = bf16[512,1024]{1,0:T(8,128)(2,1)} custom-call(s32[1]{0:T(128)} %bitcast.tm.refs_2_.refs_1_, bf16[512,512]{1,0:T(8,128)(2,1)S(1)} %shard_map.109.a01, bf16[512,512]{1,0:T(8,128)(2,1)S(1)} %collective-permute-done.11.a23, bf16[1024,1024]{1,0:T(8,128)(2,1)S(1)} %shard_map.111.w), custom_call_target="tpu_custom_call" | custom-call | flops 1000000000 | bytes 4000000 | tf_op jit(solution)/shard_map/pallas_call | solution.py:33
  (25 shorter events, 0.2 us)
Async XLA Ops:
  0.6 20.9 %copy-start = (s32[4]{0:T(128)S(1)}, s32[4]{0:T(128)}, u32[]{:S(2)}) copy-start(s32[4]{0:T(128)} %off.5) | copy-start | bytes 52
  2.5 23.0 %collective-permute-start = (bf16[384,512]{1,0:T(8,128)(2,1)S(1)}, bf16[384,512]{1,0:T(8,128)(2,1)S(1)}, u32[]{:S(2)}, u32[]{:S(2)}) collective-permute-start(bf16[384,512]{1,0:T(8,128)(2,1)S(1)} %get-tuple-element.55), channel_id=1, source_target_pairs={{0,4},{4,0},{8,12},{12,8},{16,20},{20,16},{24,28},{28,24},{32,36},... | collective-permute-start | bytes 1179656 | tf_op jit(solution)/shard_map/ppermute | solution.py:542
  3.9 9.9 %collective-permute-start.2 = (bf16[128,512]{1,0:T(8,128)(2,1)S(1)}, bf16[128,512]{1,0:T(8,128)(2,1)S(1)}, u32[]{:S(2)}, u32[]{:S(2)}) collective-permute-start(bf16[128,512]{1,0:T(8,128)(2,1)S(1)} %get-tuple-element.61), channel_id=1, source_target_pairs={{0,8},{4,12},{8,0},{12,4},{16,24},{20,28},{24,16},{28,20},{32,40},... | collective-permute-start | bytes 393224 | tf_op jit(solution)/shard_map/ppermute | solution.py:542
  5.2 7.4 %collective-permute-start.3 = (bf16[64,512]{1,0:T(8,128)(2,1)S(1)}, bf16[64,512]{1,0:T(8,128)(2,1)S(1)}, u32[]{:S(2)}, u32[]{:S(2)}) collective-permute-start(bf16[64,512]{1,0:T(8,128)(2,1)S(1)} %get-tuple-element.62), channel_id=1, source_target_pairs={{0,16},{4,20},{8,24},{12,28},{16,0},{20,4},{24,8},{28,12},{32,48},... | collective-permute-start | bytes 196616 | tf_op jit(solution)/shard_map/ppermute | solution.py:542
  7.7 6.1 %collective-permute-start.4 = (bf16[64,512]{1,0:T(8,128)(2,1)S(1)}, bf16[64,512]{1,0:T(8,128)(2,1)S(1)}, u32[]{:S(2)}, u32[]{:S(2)}) collective-permute-start(bf16[64,512]{1,0:T(8,128)(2,1)S(1)} %get-tuple-element.62), channel_id=1, source_target_pairs={{0,24},{4,28},{8,16},{12,20},{16,8},{20,12},{24,0},{28,4},{32,56},... | collective-permute-start | bytes 196616 | tf_op jit(solution)/shard_map/ppermute | solution.py:542
  13.8 11.6 %copy-start.1 = (s32[4]{0:T(128)S(1)}, s32[4]{0:T(128)}, u32[]{:S(2)}) copy-start(s32[4]{0:T(128)} %refs_1_.3) | copy-start | bytes 52
  13.8 11.0 %collective-permute-start.6 = (bf16[128,512]{1,0:T(8,128)(2,1)S(1)}, bf16[128,512]{1,0:T(8,128)(2,1)S(1)}, u32[]{:S(2)}, u32[]{:S(2)}) collective-permute-start(bf16[128,512]{1,0:T(8,128)(2,1)S(1)} %get-tuple-element.64), channel_id=1, source_target_pairs={{0,32},{4,36},{8,40},{12,44},{16,48},{20,52},{24,56},{28,60},{32,0... | collective-permute-start | bytes 393224 | tf_op jit(solution)/shard_map/ppermute | solution.py:542
  15.2 7.6 %collective-permute-start.7 = (bf16[64,512]{1,0:T(8,128)(2,1)S(1)}, bf16[64,512]{1,0:T(8,128)(2,1)S(1)}, u32[]{:S(2)}, u32[]{:S(2)}) collective-permute-start(bf16[64,512]{1,0:T(8,128)(2,1)S(1)} %get-tuple-element.65), channel_id=1, source_target_pairs={{0,64},{4,68},{8,72},{12,76},{16,80},{20,84},{24,88},{28,92},{32,9... | collective-permute-start | bytes 196616 | tf_op jit(solution)/shard_map/ppermute | solution.py:542
  17.8 6.9 %collective-permute-start.8 = (bf16[64,512]{1,0:T(8,128)(2,1)S(1)}, bf16[64,512]{1,0:T(8,128)(2,1)S(1)}, u32[]{:S(2)}, u32[]{:S(2)}) collective-permute-start(bf16[64,512]{1,0:T(8,128)(2,1)S(1)} %get-tuple-element.65), channel_id=1, source_target_pairs={{0,96},{4,100},{8,104},{12,108},{16,112},{20,116},{24,120},{28,124... | collective-permute-start | bytes 196616 | tf_op jit(solution)/shard_map/ppermute | solution.py:542
  17.8 21.8 %collective-permute-start.12 = (bf16[256,1024]{1,0:T(8,128)(2,1)S(1)}, bf16[256,1024]{1,0:T(8,128)(2,1)S(1)}, u32[]{:S(2)}, u32[]{:S(2)}) collective-permute-start(bf16[256,1024]{1,0:T(8,128)(2,1)S(1)} %get-tuple-element.51.w.own), channel_id=1, source_target_pairs={{0,1},{1,0},{2,3},{3,2},{4,7},{5,6},{6,5},{7,4},{8,9},{9,8},{10,11... | collective-permute-start | bytes 1572872 | tf_op jit(solution)/shard_map/ppermute | solution.py:550
  22.8 7.7 %collective-permute-start.1 = (bf16[256,512]{1,0:T(8,128)(2,1)S(1)}, bf16[256,512]{1,0:T(8,128)(2,1)S(1)}, u32[]{:S(2)}, u32[]{:S(2)}) collective-permute-start(bf16[256,512]{1,0:T(8,128)(2,1)S(1)} %get-tuple-element.57), channel_id=1, source_target_pairs={{4,8},{8,4},{12,16},{16,12},{20,24},{24,20},{28,32},{32,28},{36,40... | collective-permute-start | bytes 786440 | tf_op jit(solution)/shard_map/ppermute | solution.py:555
  24.7 8.3 %collective-permute-start.5 = (bf16[256,512]{1,0:T(8,128)(2,1)S(1)}, bf16[256,512]{1,0:T(8,128)(2,1)S(1)}, u32[]{:S(2)}, u32[]{:S(2)}) collective-permute-start(bf16[256,512]{1,0:T(8,128)(2,1)S(1)} %get-tuple-element.63.rest_0_), channel_id=1, source_target_pairs={{0,4},{4,0},{8,12},{12,8},{16,20},{20,16},{24,28},{28,24},{32,36},... | collective-permute-start | bytes 786440 | tf_op jit(solution)/shard_map/ppermute | solution.py:542
  24.9 8.2 %collective-permute-start.9 = (bf16[256,512]{1,0:T(8,128)(2,1)S(1)}, bf16[256,512]{1,0:T(8,128)(2,1)S(1)}, u32[]{:S(2)}, u32[]{:S(2)}) collective-permute-start(bf16[256,512]{1,0:T(8,128)(2,1)S(1)} %shard_map.107.rest_2_), channel_id=1, source_target_pairs={{0,4},{4,0},{8,12},{12,8},{16,20},{20,16},{24,28},{28,24},{32,36},... | collective-permute-start | bytes 786440 | tf_op jit(solution)/shard_map/ppermute | solution.py:542
  36.8 8.3 %collective-permute-start.18 = (bf16[512,512]{1,0:T(8,128)(2,1)S(1)}, bf16[512,512]{1,0:T(8,128)(2,1)S(1)}, u32[]{:S(2)}, u32[]{:S(2)}) collective-permute-start(bf16[512,512]{1,0:T(8,128)(2,1)S(1)} %get-tuple-element.84), channel_id=1, source_target_pairs={{0,4},{4,0},{8,12},{12,8},{16,20},{20,16},{24,28},{28,24},{32,36},... | collective-permute-start | bytes 1572872 | tf_op jit(solution)/shard_map/ppermute | solution.py:542
  36.9 7.9 %collective-permute-start.10 = (bf16[512,256]{1,0:T(8,128)(2,1)S(1)}, bf16[512,256]{1,0:T(8,128)(2,1)S(1)}, u32[]{:S(2)}, u32[]{:S(2)}) collective-permute-start(bf16[512,256]{1,0:T(8,128)(2,1)S(1)} %get-tuple-element.66.left), channel_id=1, source_target_pairs={{0,1},{1,0},{2,3},{3,2},{4,7},{5,6},{6,5},{7,4},{8,9},{9,8},{10,11... | collective-permute-start | bytes 786440 | tf_op jit(solution)/shard_map/ppermute | solution.py:550
  39.6 12.2 %collective-permute-start.14 = (bf16[128,1024]{1,0:T(8,128)(2,1)S(1)}, bf16[128,1024]{1,0:T(8,128)(2,1)S(1)}, u32[]{:S(2)}, u32[]{:S(2)}) collective-permute-start(bf16[128,1024]{1,0:T(8,128)(2,1)S(1)} %shard_map.110), channel_id=1, source_target_pairs={{0,3},{1,2},{2,1},{3,0},{4,5},{5,4},{6,7},{7,6},{8,11},{9,10},{10,... | collective-permute-start | bytes 786440 | tf_op jit(solution)/shard_map/ppermute | solution.py:550
  39.7 30.6 %collective-permute-start.13 = (bf16[256,1024]{1,0:T(8,128)(2,1)S(1)}, bf16[256,1024]{1,0:T(8,128)(2,1)S(1)}, u32[]{:S(2)}, u32[]{:S(2)}) collective-permute-start(bf16[256,1024]{1,0:T(8,128)(2,1)S(1)} %collective-permute-done.12.w.first), channel_id=1, source_target_pairs={{0,4},{4,0},{8,12},{12,8},{16,20},{20,16},{24,28},{28,24},{32,36},... | collective-permute-start | bytes 1572872 | tf_op jit(solution)/shard_map/ppermute | solution.py:542
  44.8 32.0 %collective-permute-start.11 = (bf16[512,512]{1,0:T(8,128)(2,1)S(1)}, bf16[512,512]{1,0:T(8,128)(2,1)S(1)}, u32[]{:S(2)}, u32[]{:S(2)}) collective-permute-start(bf16[512,512]{1,0:T(8,128)(2,1)S(1)} %shard_map.109.a01), channel_id=1, source_target_pairs={{0,3},{1,2},{2,1},{3,0},{4,5},{5,4},{6,7},{7,6},{8,11},{9,10},{10,... | collective-permute-start | bytes 1572872 | tf_op jit(solution)/shard_map/ppermute | solution.py:550
  45.2 15.8 %collective-permute-start.19 = (bf16[128,512]{1,0:T(8,128)(2,1)S(1)}, bf16[128,512]{1,0:T(8,128)(2,1)S(1)}, u32[]{:S(2)}, u32[]{:S(2)}) collective-permute-start(bf16[128,512]{1,0:T(8,128)(2,1)S(1)} %get-tuple-element.85), channel_id=1, source_target_pairs={{0,32},{4,36},{8,40},{12,44},{16,48},{20,52},{24,56},{28,60},{32,0... | collective-permute-start | bytes 393224 | tf_op jit(solution)/shard_map/ppermute | solution.py:542
  49.2 5.7 %collective-permute-start.20 = (bf16[64,512]{1,0:T(8,128)(2,1)S(1)}, bf16[64,512]{1,0:T(8,128)(2,1)S(1)}, u32[]{:S(2)}, u32[]{:S(2)}) collective-permute-start(bf16[64,512]{1,0:T(8,128)(2,1)S(1)} %get-tuple-element.86), channel_id=1, source_target_pairs={{0,64},{4,68},{8,72},{12,76},{16,80},{20,84},{24,88},{28,92},{32,9... | collective-permute-start | bytes 196616 | tf_op jit(solution)/shard_map/ppermute | solution.py:542
  51.8 7.2 %collective-permute-start.21 = (bf16[64,512]{1,0:T(8,128)(2,1)S(1)}, bf16[64,512]{1,0:T(8,128)(2,1)S(1)}, u32[]{:S(2)}, u32[]{:S(2)}) collective-permute-start(bf16[64,512]{1,0:T(8,128)(2,1)S(1)} %get-tuple-element.87), channel_id=1, source_target_pairs={{0,96},{4,100},{8,104},{12,108},{16,112},{20,116},{24,120},{28,124... | collective-permute-start | bytes 196616 | tf_op jit(solution)/shard_map/ppermute | solution.py:542
  54.9 15.8 %collective-permute-start.16 = (bf16[384,512]{1,0:T(8,128)(2,1)S(1)}, bf16[384,512]{1,0:T(8,128)(2,1)S(1)}, u32[]{:S(2)}, u32[]{:S(2)}) collective-permute-start(bf16[384,512]{1,0:T(8,128)(2,1)S(1)} %get-tuple-element.81), channel_id=1, source_target_pairs={{0,4},{4,0},{8,12},{12,8},{16,20},{20,16},{24,28},{28,24},{32,36},... | collective-permute-start | bytes 1179656 | tf_op jit(solution)/shard_map/ppermute | solution.py:542
  59.1 7.7 %collective-permute-start.17 = (bf16[256,512]{1,0:T(8,128)(2,1)S(1)}, bf16[256,512]{1,0:T(8,128)(2,1)S(1)}, u32[]{:S(2)}, u32[]{:S(2)}) collective-permute-start(bf16[256,512]{1,0:T(8,128)(2,1)S(1)} %get-tuple-element.82), channel_id=1, source_target_pairs={{4,8},{8,4},{12,16},{16,12},{20,24},{24,20},{28,32},{32,28},{36,40... | collective-permute-start | bytes 786440 | tf_op jit(solution)/shard_map/ppermute | solution.py:555
  61.0 5.8 %collective-permute-start.15 = (bf16[128,1024]{1,0:T(8,128)(2,1)S(1)}, bf16[128,1024]{1,0:T(8,128)(2,1)S(1)}, u32[]{:S(2)}, u32[]{:S(2)}) collective-permute-start(bf16[128,1024]{1,0:T(8,128)(2,1)S(1)} %collective-permute-done.14.mine), channel_id=1, source_target_pairs={{0,4},{4,0},{8,12},{12,8},{16,20},{20,16},{24,28},{28,24},{32,36},... | collective-permute-start | bytes 786440 | tf_op jit(solution)/shard_map/ppermute | solution.py:542
  66.8 8.2 %collective-permute-start.22 = (bf16[128,512]{1,0:T(8,128)(2,1)S(1)}, bf16[128,512]{1,0:T(8,128)(2,1)S(1)}, u32[]{:S(2)}, u32[]{:S(2)}) collective-permute-start(bf16[128,512]{1,0:T(8,128)(2,1)S(1)} %get-tuple-element.89), channel_id=1, source_target_pairs={{0,8},{4,12},{8,0},{12,4},{16,24},{20,28},{24,16},{28,20},{32,40},... | collective-permute-start | bytes 393224 | tf_op jit(solution)/shard_map/ppermute | solution.py:542
  66.8 7.4 %collective-permute-start.23 = (bf16[64,512]{1,0:T(8,128)(2,1)S(1)}, bf16[64,512]{1,0:T(8,128)(2,1)S(1)}, u32[]{:S(2)}, u32[]{:S(2)}) collective-permute-start(bf16[64,512]{1,0:T(8,128)(2,1)S(1)} %get-tuple-element.90), channel_id=1, source_target_pairs={{0,16},{4,20},{8,24},{12,28},{16,0},{20,4},{24,8},{28,12},{32,48},... | collective-permute-start | bytes 196616 | tf_op jit(solution)/shard_map/ppermute | solution.py:542
  70.3 4.7 %collective-permute-start.24 = (bf16[64,512]{1,0:T(8,128)(2,1)S(1)}, bf16[64,512]{1,0:T(8,128)(2,1)S(1)}, u32[]{:S(2)}, u32[]{:S(2)}) collective-permute-start(bf16[64,512]{1,0:T(8,128)(2,1)S(1)} %get-tuple-element.91), channel_id=1, source_target_pairs={{0,24},{4,28},{8,16},{12,20},{16,8},{20,12},{24,0},{28,4},{32,56},... | collective-permute-start | bytes 196616 | tf_op jit(solution)/shard_map/ppermute | solution.py:542
